TPU v7x, 512 devices: a whole 4x8x8 slice. The times are simulated.
512 devices in a mesh: wa: 32 (over y, x_hi, core), gz: 16 (over x_lo, z).
Axes of the slice: x: 4 (x_hi: 2, x_lo: 2; x = x_hi * 2 + x_lo), y: 8, z: 8, core: 2. Of those that a mesh axis runs over, the one named last changes fastest.
Arguments:
- velocity_modes: float32 [2, 32, 512, 512], P(None, 'gz', 'wa'), may hold values from -0.03125 to 0.03125
- scalar: float32 [64, 1024, 1024], P('gz', 'wa'), may hold values from -3 to 3
- nest_shift: int32 [1], replicated, may hold values from 0 to 1023
Outputs:
- stress: bfloat16 [2, 32, 512, 512], P(None, 'gz', 'wa')
- scalar_next: float32 [64, 1024, 1024], P('gz', 'wa')
Inputs may be any that keep to these rules, and one draw needn't show every extreme that they name: `nest_shift`: a shift of the fine grid along x in fine cells.
All inputs are finite; a program needn't handle non-finite values.
Results may differ from a plain program's by a relative error of at most 0.001.
Values sent between devices are 32-bit elements; how exact they have to be, the bound alone decides.
No kernel may reach another device: no remote copies, remote signals or barrier semaphores. Data moves between devices by JAX's collectives and lax.ppermute only.
A program may use at most 64 MiB of HBM per device.

v0:
```python
import math

import jax
import jax.numpy as jnp
import ml_dtypes
import numpy as np
from jax import lax
from jax.experimental import pallas as pl
from jax.experimental.pallas import tpu as pltpu
from jax.sharding import PartitionSpec as P


F32 = jnp.float32
BF16 = jnp.bfloat16
N = 768
HALF = 256
OWN = 24
ROWS = 32
EXT = 40
RETAINED = (0, 1, 4, 5)
BASE = 512
PAYLOAD = BASE + 2 * 8 * EXT + 8


def split_host(array):
    high = array.astype(np.float32).astype(ml_dtypes.bfloat16)
    low = (array - high.astype(np.float64)).astype(np.float32).astype(ml_dtypes.bfloat16)
    return high, low


def cas_seeds():
    lane = np.arange(128, dtype=np.int64)
    rows = []
    for steps in (8 * np.arange(96, dtype=np.int64), np.arange(8, dtype=np.int64)):
        angle = ((steps[:, None] * lane) % N).astype(np.float64) * (2.0 * math.pi / N)
        rows += [np.cos(angle), np.sin(angle)]
    return np.concatenate(rows).astype(np.float32)


def weights_of(t):
    return (
        (-(t**3) + 2 * t**2 - t) / 2,
        (3 * t**3 - 5 * t**2 + 2) / 2,
        (-3 * t**3 + 4 * t**2 + t) / 2,
        (t**3 - t**2) / 2,
    )


def row_plane_matrix():
    along_y = np.zeros((EXT, ROWS))
    for e in range(1, 35):
        numer = 3 * (2 * (e - 2) + 1)
        for offset, weight in zip(range(-1, 3), weights_of((numer % 8) / 8.0)):
            along_y[e, numer // 8 + offset + 2] += weight
    along_z = np.zeros((6, 6))
    for k in range(6):
        numer = 2 * (k - 1) - 1
        for offset, weight in zip(range(-1, 3), weights_of((numer % 4) / 4.0)):
            along_z[k, numer // 4 + offset + 2] += weight
    full = np.einsum("kp,er->kepr", along_z, along_y).reshape(6 * EXT, 6, ROWS)
    below, own, above = (full[:, i : i + 2].reshape(6 * EXT, 64) for i in (0, 2, 4))
    none = np.zeros_like(own)
    return np.stack(
        [
            np.concatenate([below, above, own, none], axis=1),
            np.concatenate([below, above, none, own], axis=1),
        ]
    )


def mm(a, b):
    return lax.dot_general(a, b, (((1,), (0,)), ((), ())), preferred_element_type=F32)


def mm_nt(a, b):
    return lax.dot_general(a, b, (((1,), (1,)), ((), ())), preferred_element_type=F32)


def split(x):
    high = x.astype(BF16)
    low = (x - high.astype(F32)).astype(BF16)
    return high, low


def lanes_of(shape):
    return lax.broadcasted_iota(jnp.int32, shape, len(shape) - 1)


def make_table(seed_ref, fh_ref, fl_ref, blocks=(0, 1, 2, 3, 4, 5)):
    near_cos, near_sin = seed_ref[192:200, :], seed_ref[200:208, :]
    sublane = lax.broadcasted_iota(jnp.int32, (8, 128), 0)
    turns = []
    for phase in range(3):
        turns.append([])
        for b in range(6):
            sixth = lax.rem(b * (2 * phase + sublane), 6)
            cos, sin = jnp.ones((8, 128), F32), jnp.zeros((8, 128), F32)
            for i in range(1, 6):
                angle = 2.0 * math.pi * i / 6
                cos = jnp.where(sixth == i, round(math.cos(angle), 6), cos)
                sin = jnp.where(sixth == i, 0.0 if i == 3 else math.sin(angle), sin)
            turns[-1].append((cos, sin))

    def six(step, carry):
        for pair in range(3):
            parts = []
            for i in (2 * pair, 2 * pair + 1):
                m = 6 * step + i
                far_cos, far_sin = seed_ref[pl.ds(m, 1), :], seed_ref[pl.ds(96 + m, 1), :]
                cos = far_cos * near_cos - far_sin * near_sin
                sin = far_sin * near_cos + far_cos * near_sin
                plus, minus = cos + sin, cos - sin
                tiles = []
                for b in blocks:
                    turn_cos, turn_sin = turns[i % 3][b]
                    tiles.append(turn_cos * plus + turn_sin * minus if b else plus)
                parts.append(jnp.concatenate(tiles, axis=1))
            high, low = split(jnp.concatenate(parts, axis=0))
            row = pl.multiple_of(48 * step + 16 * pair, 16)
            fh_ref[pl.ds(row, 16), :] = high
            fl_ref[pl.ds(row, 16), :] = low
        return carry

    lax.fori_loop(0, 16, six, 0)


def synth_y_kernel(m_ref, seed_ref, out_ref, fh_ref, fl_ref):
    make_table(seed_ref, fh_ref, fl_ref)
    mh, ml = split(m_ref[...])
    both = jnp.concatenate([mh, ml], axis=0)
    stacked = mm(both[:, :HALF], fh_ref[0:HALF, :]) + mm(both[:, HALF:], fh_ref[512:, :])
    lines = stacked[:64] + stacked[64:]
    lines = lines + mm(mh[:, :HALF], fl_ref[0:HALF, :]) + mm(mh[:, HALF:], fl_ref[512:, :])
    tiles = [lines[:, 128 * t : 128 * t + 128] for t in range(6)]
    lane = lanes_of((64, 128))
    group = lanes_of((16, 128)) // 32
    for d in range(32):
        start = (OWN * d - 2) % N
        t, first = start // 128, start % 128
        window = tiles[t]
        if first + ROWS > 128:
            window = jnp.where(lane >= first, window, tiles[(t + 1) % 6])
        chunk = None
        for cz in range(4):
            piece = window[16 * cz : 16 * cz + 16]
            shift = (32 * cz - first) % 128
            if shift:
                piece = pltpu.roll(piece, shift, 1)
            chunk = piece if chunk is None else jnp.where(group == cz, piece, chunk)
        out_ref[16 * d : 16 * d + 16, :] = chunk


def pack_kernel(r_ref, g_ref, before_ref, after_ref, up_ref, down_ref):
    received = r_ref[...]
    for ref in (up_ref, down_ref):
        ref[0:BASE, :] = received
        ref[PAYLOAD - 8 : PAYLOAD, :] = jnp.zeros((8, 128), F32)
    for p in range(4):
        ref = down_ref if p < 2 else up_ref
        for t in range(8):
            row = BASE + ((p % 2) * 8 + t) * EXT
            columns = slice(128 * t, 128 * t + 128)
            ref[row : row + 2, :] = before_ref[2 * p : 2 * p + 2, columns]
            ref[row + 2 : row + 34, :] = g_ref[p, :, columns]
            ref[row + 34 : row + 36, :] = after_ref[2 * p : 2 * p + 2, columns]
            ref[row + 36 : row + 40, :] = jnp.zeros((4, 128), F32)


def spectral_kernel(r_ref, seed_ref, spaced_ref, out_ref, fh_ref, fl_ref):
    make_table(seed_ref, fh_ref, fl_ref)
    rh, rl = split(r_ref[0:BASE, :])
    both = jnp.concatenate([rh, rl], axis=1)
    o = mm(fh_ref[:, 0:HALF], both[0:HALF]) + mm(fh_ref[:, 512:], both[HALF:])
    spaced = o[:, :128] + o[:, 128:]
    spaced = spaced + mm(fl_ref[:, 0:HALF], rh[0:HALF]) + mm(fl_ref[:, 512:], rh[HALF:])
    spaced_ref[...] = spaced
    swapped = pltpu.roll(spaced, 64, 1)
    products = jnp.where(
        lanes_of((N, 128)) < 64,
        spaced * spaced - swapped * swapped,
        spaced * swapped,
    )
    ph, plo = split(products)
    both = jnp.concatenate([ph, plo], axis=1)
    for first, row in ((0, 0), (512, HALF)):
        o = mm(fh_ref[first : first + HALF, :], both)
        out_ref[row : row + HALF, :] = (
            o[:, :128] + o[:, 128:] + mm(fl_ref[first : first + HALF, :], ph)
        )


def analysis_y_kernel(r_ref, seed_ref, out_ref, fh_ref, fl_ref):
    make_table(seed_ref, fh_ref, fl_ref, RETAINED)
    lane = lanes_of((16, 128))
    columns = []
    for t in range(6):
        rows = []
        for cz in range(4):
            tile = None
            for d in range(32):
                low, high = OWN * d - 128 * t, OWN * d - 128 * t + OWN
                if high <= 0 or low >= 128:
                    continue
                shift = (low - (32 * cz + 2)) % 128
                piece = r_ref[16 * d : 16 * d + 16, :]
                if shift:
                    piece = pltpu.roll(piece, shift, 1)
                tile = piece if tile is None else jnp.where(lane >= low, piece, tile)
            rows.append(tile)
        columns.append(jnp.concatenate(rows, axis=0))
    lines = jnp.concatenate(columns, axis=1)
    ah, al = split(lines)
    both = jnp.concatenate([ah, al], axis=0)
    o = mm(both, fh_ref[...])
    o = o[:64] + o[64:] + mm(ah, fl_ref[...])
    out_ref[...] = (o * (1.0 / N)).astype(BF16)


def flux(g, gg, h, hh):
    return (h - g) * (gg + hh)


def fine_kernel(
    shift_ref,
    spaced_ref,
    up_ref,
    down_ref,
    low_ref,
    high_ref,
    seed_ref,
    bh_ref,
    bl_ref,
    out_ref,
    fh_ref,
    fl_ref,
    x_ref,
    u_ref,
    s_ref,
):
    make_table(seed_ref, fh_ref, fl_ref, RETAINED)
    below = low_ref[0:BASE, :]
    above = high_ref[0:BASE, :]
    left = lanes_of((BASE, 128)) < 64
    first = jnp.where(left, below, pltpu.roll(above, 64, 1))
    second = jnp.where(left, pltpu.roll(below, 64, 1), above)
    rh, rl = split(jnp.concatenate([first, second], axis=1))
    halo = mm(fh_ref[...], rh) + mm(fh_ref[...], rl) + mm(fl_ref[...], rh)
    for i, tile in enumerate((halo[:, :128], halo[:, 128:], spaced_ref[...])):
        x_ref[i, 0:N, :] = tile
        x_ref[i, N : N + 128, :] = tile[0:128]

    shift = shift_ref[0]
    base = lax.shift_right_arithmetic(3 * (1 + 2 * shift), 3) - 1
    cell = lax.broadcasted_iota(jnp.int32, (128, 128), 0)
    coarse = lanes_of((128, 128))
    numer = 3 * (2 * cell + 1 + 2 * shift)
    lower = lax.shift_right_arithmetic(numer, 3) - base
    t = jnp.bitwise_and(numer, 7).astype(F32) * 0.125
    square = t * t
    cube = square * t
    weights = (
        (-cube + 2.0 * square - t) * 0.5,
        (3.0 * cube - 5.0 * square + 2.0) * 0.5,
        (-3.0 * cube + 4.0 * square + t) * 0.5,
        (cube - square) * 0.5,
    )
    matrix = jnp.zeros((128, 128), F32)
    for offset, weight in zip(range(-1, 3), weights):
        matrix = matrix + jnp.where(coarse == lower + offset, weight, 0.0)
    wh, wl = split(matrix)
    both = jnp.concatenate([wh, wl], axis=0)

    for pair in range(4):
        lines = []
        for b in (2 * pair, 2 * pair + 1):
            start = lax.rem(base + N + 96 * b, N)
            window = jnp.concatenate([x_ref[i, pl.ds(start, 128), :] for i in range(3)], axis=1)
            vh, vl = split(window)
            o = mm(both, vh)
            lines.append(o[:128] + o[128:] + mm(wh, vl))
        lines = jnp.concatenate(lines, axis=0)
        for c in range(2):
            mine = jnp.concatenate([lines[:, 128 * c : 128 * c + 128], lines[:, 256:]], axis=1)
            vh, vl = split(mine)
            o = mm_nt(bh_ref[c], vh) + mm_nt(bl_ref[c], vh) + mm_nt(bh_ref[c], vl)
            u_ref[c, 2 * pair] = o[:, :128]
            u_ref[c, 2 * pair + 1] = o[:, 128:]

    homes = ((low_ref, 0), (low_ref, 1), (down_ref, 0), (down_ref, 1))
    homes = homes + ((up_ref, 0), (up_ref, 1), (high_ref, 0), (high_ref, 1))

    def around(centre, west, east):
        lane = lanes_of(centre.shape)
        to_east = jnp.where(lane == 127, pltpu.roll(east, 127, 1), pltpu.roll(centre, 127, 1))
        to_west = jnp.where(lane == 0, pltpu.roll(west, 1, 1), pltpu.roll(centre, 1, 1))
        return to_west, to_east

    def rate(load, planes, count, skip, use):
        def one(t, carry):
            west_t = lax.rem(t + 7, 8)
            east_t = lax.rem(t + 1, 8)
            first = planes[0]
            g = load(first, t, skip, count)
            gg = 1.0 + g * g
            below = load(first - 1, t, skip, count)
            lower = flux(below, 1.0 + below * below, g, gg)
            for p in planes:
                above = load(p + 1, t, skip, count)
                aa = 1.0 + above * above
                upper = flux(g, gg, above, aa)
                north = load(p, t, skip + 1, count)
                south = load(p, t, skip - 1, count)
                west, east = around(
                    g, load(p, west_t, skip, count), load(p, east_t, skip, count)
                )
                total = flux(g, gg, north, 1.0 + north * north) + flux(
                    g, gg, south, 1.0 + south * south
                )
                total = total + flux(g, gg, east, 1.0 + east * east)
                total = total + flux(g, gg, west, 1.0 + west * west)
                total = total + upper - lower
                row = (p - 1) * EXT + skip
                along_x = u_ref[0, t, row : row + count, :]
                along_y = u_ref[1, t, row : row + count, :]
                wind = along_x * (east - west) + along_y * (north - south)
                use(p, t, g, g + (0.01 * total - 0.1 * wind))
                lower, g, gg = upper, above, aa
            return carry

        lax.fori_loop(0, 8, one, 0)

    def load_scalar(p, t, skip, count):
        ref, plane = homes[p]
        row = pl.multiple_of(BASE + (plane * 8 + t) * EXT, 8)
        return ref[pl.ds(row + skip, count), :]

    def load_section(p, t, skip, count):
        row = pl.multiple_of(((p - 1) * 8 + t) * EXT, 8)
        return s_ref[pl.ds(row + skip, count), :]

    def keep_section(p, t, g, result):
        row = pl.multiple_of(((p - 1) * 8 + t) * EXT, 8)
        s_ref[pl.ds(row, EXT), :] = result

    def keep_result(p, t, g, result):
        scalar = load_scalar(p, t, 2, 32)
        column = pl.multiple_of(t * 128, 128)
        out_ref[p - 2, :, pl.ds(column, 128)] = 0.5 * (scalar + result)

    rate(load_scalar, range(1, 7), EXT, 0, keep_section)
    rate(load_section, range(2, 6), 32, 2, keep_result)


def call(kernel, outs, flops, limit, scratch=(), smem=0):
    vmem = pl.BlockSpec(memory_space=pltpu.VMEM)

    def run(*args):
        specs = [pl.BlockSpec(memory_space=pltpu.SMEM)] * smem + [vmem] * (len(args) - smem)
        size = sum(math.prod(a.shape) * a.dtype.itemsize for a in args)
        return pl.pallas_call(
            kernel,
            out_shape=outs,
            in_specs=specs,
            out_specs=jax.tree.map(lambda _: vmem, outs),
            scratch_shapes=scratch,
            compiler_params=pltpu.CompilerParams(vmem_limit_bytes=limit * 2**20),
            cost_estimate=pl.CostEstimate(flops=flops, bytes_accessed=size, transcendentals=0),
        )(*args)

    return run


def shards(velocity_modes, scalar, nest_shift):
    bh, bl = (jnp.asarray(a) for a in split_host(row_plane_matrix()))
    of = jax.ShapeDtypeStruct

    def ring(axis):
        count = lax.axis_size(axis)
        up = [(i, (i + 1) % count) for i in range(count)]
        return up, [(b, a) for a, b in up]

    def exchange(block):
        block = block.reshape(32, 16, 128)
        return lax.all_to_all(block, "wa", split_axis=0, concat_axis=0, tiled=True).reshape(512, 128)

    modes = velocity_modes.reshape(64, 512)
    seeds = jnp.asarray(cas_seeds())
    full = (pltpu.VMEM((N, N), BF16),) * 2
    retained = (pltpu.VMEM((N, 512), BF16),) * 2
    sent = call(synth_y_kernel, of((512, 128), F32), 10**9, 12, scratch=full)(modes, seeds)
    received = exchange(sent)

    up, down = ring("wa")
    before = lax.ppermute(scalar[:, 30:32, :].reshape(8, 1024), "wa", up)
    after = lax.ppermute(scalar[:, 0:2, :].reshape(8, 1024), "wa", down)

    payload = of((PAYLOAD, 128), F32)
    to_up, to_down = call(pack_kernel, (payload, payload), 10**6, 8)(
        received, scalar, before, after
    )
    up, down = ring("gz")
    from_low = lax.ppermute(to_up, "gz", up)
    from_high = lax.ppermute(to_down, "gz", down)

    spaced, half = call(
        spectral_kernel, (of((N, 128), F32), of((512, 128), F32)), 10**9, 12, scratch=full
    )(to_up, seeds)
    returned = exchange(half)

    scalar_next = call(
        fine_kernel,
        of((4, 32, 1024), F32),
        2 * 10**9,
        24,
        scratch=retained
        + (
            pltpu.VMEM((3, N + 128, 128), F32),
            pltpu.VMEM((2, 8, 6 * EXT, 128), F32),
            pltpu.VMEM((6 * 8 * EXT + 8, 128), F32),
        ),
        smem=1,
    )(nest_shift, spaced, to_up, to_down, from_low, from_high, seeds, bh, bl)

    stress = call(
        analysis_y_kernel, of((64, 512), BF16), 10**9, 8, scratch=retained
    )(returned, seeds)
    return (stress.reshape(2, 2, 16, 512), scalar_next)


def solution(mesh):
    placed = (P(None, "gz", "wa", None), P("gz", "wa", None), P())
    return jax.shard_map(
        shards,
        mesh=mesh,
        in_specs=placed,
        out_specs=(P(None, "gz", "wa", None), P("gz", "wa", None)),
        check_vma=False,
    )
```

profile of v0, /device:TPU:12, one launch (start us, length us, event | category | flops | bytes accessed | tf_op | source)
XLA Modules:
  0.0 75.5 jit_solution(12088431280832006630)
XLA Ops:
  0.6 0.9 %copy-done.1 = f32[2,2,16,512]{3,2,1,0:T(8,128)S(1)} copy-done((f32[2,2,16,512]{3,2,1,0:T(8,128)S(1)}, f32[2,2,16,512]{3,2,1,0:T(8,128)}, u32[]{:S(2)}) %copy-start.1) | copy-done | bytes 131096
  1.5 0.9 %copy-done.4 = f32[208,128]{1,0:T(8,128)S(1)} copy-done((f32[208,128]{1,0:T(8,128)S(1)}, f32[208,128]{1,0:T(8,128)}, u32[]{:S(2)}) %copy-start.4) | copy-done | bytes 106520
  2.4 2.1 %shard_map.77 = f32[512,128]{1,0:T(8,128)} custom-call(f32[64,512]{1,0:T(8,128)S(1)} %bitcast.8, f32[208,128]{1,0:T(8,128)S(1)} %copy-done.4), custom_call_target="tpu_custom_call" | custom-call | flops 1000000000 | bytes 237568 | tf_op jit(solution)/shard_map/pallas_call | solution.py:360
  4.5 10.3 %all-to-all-start = ((f32[32,16,128]{2,1,0:T(8,128)}), f32[32,16,128]{2,1,0:T(8,128)S(1)}, u32[]{:S(2)}, u32[]{:S(2)}) async-start(f32[32,16,128]{2,1,0:T(8,128)} %bitcast.1), calls=%async_computation | async-start | bytes 524288 | tf_op jit(solution)/shard_map/all_to_all | solution.py:384
  14.9 2.0 %collective-permute-start = (f32[8,1024]{1,0:T(8,128)S(1)}, f32[8,1024]{1,0:T(8,128)S(1)}, u32[]{:S(2)}, u32[]{:S(2)}) collective-permute-start(f32[8,1024]{1,0:T(8,128)S(1)} %reshape.31), channel_id=1, source_target_pairs={{0,16},{16,32},{32,48},{48,64},{64,80},{80,96},{96,112},{112,128},... | collective-permute-start | bytes 98312 | tf_op jit(solution)/shard_map/ppermute | solution.py:394
  16.9 5.0 %collective-permute-start.1 = (f32[8,1024]{1,0:T(8,128)S(1)}, f32[8,1024]{1,0:T(8,128)S(1)}, u32[]{:S(2)}, u32[]{:S(2)}) collective-permute-start(f32[8,1024]{1,0:T(8,128)S(1)} %reshape.32), channel_id=1, source_target_pairs={{16,0},{32,16},{48,32},{64,48},{80,64},{96,80},{112,96},{128,112},... | collective-permute-start | bytes 98312 | tf_op jit(solution)/shard_map/ppermute | solution.py:395
  22.0 0.1 collective-permute-done.before_ref
  22.1 1.5 %collective-permute-done.1.after_ref = f32[8,1024]{1,0:T(8,128)S(1)} collective-permute-done((f32[8,1024]{1,0:T(8,128)S(1)}, f32[8,1024]{1,0:T(8,128)S(1)}, u32[]{:S(2)}, u32[]{:S(2)}) %collective-permute-start.1) | collective-permute-done | bytes 32800 | tf_op jit(solution)/shard_map/ppermute | solution.py:395
  23.6 2.4 %all-to-all-done = f32[32,16,128]{2,1,0:T(8,128)S(1)} async-done(((f32[32,16,128]{2,1,0:T(8,128)}), f32[32,16,128]{2,1,0:T(8,128)S(1)}, u32[]{:S(2)}, u32[]{:S(2)}) %all-to-all-start) | async-done | bytes 262176 | tf_op jit(solution)/shard_map/all_to_all | solution.py:384
  26.0 0.1 shard_map.78
  26.1 0.8 %copy-done.5 = f32[208,128]{1,0:T(8,128)S(1)} copy-done((f32[208,128]{1,0:T(8,128)S(1)}, f32[208,128]{1,0:T(8,128)}, u32[]{:S(2)}) %copy-start.5) | copy-done | bytes 106520
  26.9 2.5 %shard_map.79 = (f32[768,128]{1,0:T(8,128)S(1)}, f32[512,128]{1,0:T(8,128)}) custom-call(f32[1160,128]{1,0:T(8,128)S(1)} %get-tuple-element.6.r_ref.up_ref, f32[208,128]{1,0:T(8,128)S(1)} %copy-done.5), custom_call_target="tpu_custom_call" | custom-call | flops 1000000000 | bytes 700416 | tf_op jit(solution)/shard_map/pallas_call | solution.py:360
  29.4 0.7 copy-done.6
  30.1 9.7 %all-to-all-start.1 = ((f32[32,16,128]{2,1,0:T(8,128)}), f32[32,16,128]{2,1,0:T(8,128)S(1)}, u32[]{:S(2)}, u32[]{:S(2)}) async-start(f32[32,16,128]{2,1,0:T(8,128)} %bitcast.3), calls=%async_computation.1 | async-start | bytes 524288 | tf_op jit(solution)/shard_map/all_to_all | solution.py:384
  39.9 4.3 %collective-permute-start.2 = (f32[1160,128]{1,0:T(8,128)S(1)}, f32[1160,128]{1,0:T(8,128)S(1)}, u32[]{:S(2)}, u32[]{:S(2)}) collective-permute-start(f32[1160,128]{1,0:T(8,128)S(1)} %get-tuple-element.6.r_ref.up_ref), channel_id=1, source_target_pairs={{0,1},{1,2},{2,3},{3,4},{4,5},{5,6},{6,7},{7,8},{8,9},{9,10},{10,1... | collective-permute-start | bytes 1781768 | tf_op jit(solution)/shard_map/ppermute | solution.py:402
  44.2 9.2 %collective-permute-start.3 = (f32[1160,128]{1,0:T(8,128)S(1)}, f32[1160,128]{1,0:T(8,128)S(1)}, u32[]{:S(2)}, u32[]{:S(2)}) collective-permute-start(f32[1160,128]{1,0:T(8,128)S(1)} %get-tuple-element.9.down_ref), channel_id=1, source_target_pairs={{1,0},{2,1},{3,2},{4,3},{5,4},{6,5},{7,6},{8,7},{9,8},{10,9},{11,1... | collective-permute-start | bytes 1781768 | tf_op jit(solution)/shard_map/ppermute | solution.py:403
  54.1 0.0 all-to-all-done.1
  54.1 0.0 copy-start.2
  54.1 0.0 copy-start.3
  54.1 0.0 copy-start.7
  54.1 1.8 %shard_map.80 = bf16[64,512]{1,0:T(8,128)(2,1)} custom-call(f32[512,128]{1,0:T(8,128)S(1)} %bitcast.7, f32[208,128]{1,0:T(8,128)S(1)} %copy-done.5), custom_call_target="tpu_custom_call" | custom-call | flops 1000000000 | bytes 368640 | tf_op jit(solution)/shard_map/pallas_call | solution.py:360
  55.9 9.3 %collective-permute-done.2.low_ref = f32[1160,128]{1,0:T(8,128)S(1)} collective-permute-done((f32[1160,128]{1,0:T(8,128)S(1)}, f32[1160,128]{1,0:T(8,128)S(1)}, u32[]{:S(2)}, u32[]{:S(2)}) %collective-permute-start.2) | collective-permute-done | bytes 593952 | tf_op jit(solution)/shard_map/ppermute | solution.py:402
  65.2 1.6 %collective-permute-done.3.high_ref = f32[1160,128]{1,0:T(8,128)S(1)} collective-permute-done((f32[1160,128]{1,0:T(8,128)S(1)}, f32[1160,128]{1,0:T(8,128)S(1)}, u32[]{:S(2)}, u32[]{:S(2)}) %collective-permute-start.3) | collective-permute-done | bytes 593952 | tf_op jit(solution)/shard_map/ppermute | solution.py:403
  66.7 8.8 %shard_map.81 = f32[4,32,1024]{2,1,0:T(8,128)} custom-call(s32[1]{0:T(128)S(6)} %copy.8.shift_ref, f32[768,128]{1,0:T(8,128)S(1)} %copy-done.7, f32[1160,128]{1,0:T(8,128)S(1)} %get-tuple-element.6.r_ref.up_ref, f32[1160,128]{1,0:T(8,128)S(1)} %get-tuple-element.9.down_ref, f32[1160,128]{1,0:T(8,128)S(1)} %collective-permute-done.2.low_ref, ...), custom_call_target="tpu_custom_call" | custom-call | flops 2000000000 | bytes 3366916 | tf_op jit(solution)/shard_map/pallas_call | solution.py:360
  (12 shorter events, 0.1 us)
Async XLA Ops:
  0.6 0.9 %copy-start.1 = (f32[2,2,16,512]{3,2,1,0:T(8,128)S(1)}, f32[2,2,16,512]{3,2,1,0:T(8,128)}, u32[]{:S(2)}) copy-start(f32[2,2,16,512]{3,2,1,0:T(8,128)} %param.6) | copy-start | bytes 393220
  1.5 0.9 %copy-start.4 = (f32[208,128]{1,0:T(8,128)S(1)}, f32[208,128]{1,0:T(8,128)}, u32[]{:S(2)}) copy-start(f32[208,128]{1,0:T(8,128)} %constant.8.clone.seed_ref) | copy-start | bytes 319492
  4.5 10.3 %copy-start = (f32[4,32,1024]{2,1,0:T(8,128)S(1)}, f32[4,32,1024]{2,1,0:T(8,128)}, u32[]{:S(2)}) copy-start(f32[4,32,1024]{2,1,0:T(8,128)} %g_ref.1) | copy-start | bytes 1572868
  4.5 21.4 %all-to-all-start = ((f32[32,16,128]{2,1,0:T(8,128)}), f32[32,16,128]{2,1,0:T(8,128)S(1)}, u32[]{:S(2)}, u32[]{:S(2)}) async-start(f32[32,16,128]{2,1,0:T(8,128)} %bitcast.1), calls=%async_computation | async-start | bytes 524288 | tf_op jit(solution)/shard_map/all_to_all | solution.py:384
  14.9 7.2 %collective-permute-start = (f32[8,1024]{1,0:T(8,128)S(1)}, f32[8,1024]{1,0:T(8,128)S(1)}, u32[]{:S(2)}, u32[]{:S(2)}) collective-permute-start(f32[8,1024]{1,0:T(8,128)S(1)} %reshape.31), channel_id=1, source_target_pairs={{0,16},{16,32},{32,48},{48,64},{64,80},{80,96},{96,112},{112,128},... | collective-permute-start | bytes 98312 | tf_op jit(solution)/shard_map/ppermute | solution.py:394
  16.9 6.6 %collective-permute-start.1 = (f32[8,1024]{1,0:T(8,128)S(1)}, f32[8,1024]{1,0:T(8,128)S(1)}, u32[]{:S(2)}, u32[]{:S(2)}) collective-permute-start(f32[8,1024]{1,0:T(8,128)S(1)} %reshape.32), channel_id=1, source_target_pairs={{16,0},{32,16},{48,32},{64,48},{80,64},{96,80},{112,96},{128,112},... | collective-permute-start | bytes 98312 | tf_op jit(solution)/shard_map/ppermute | solution.py:395
  26.0 0.9 %copy-start.5 = (f32[208,128]{1,0:T(8,128)S(1)}, f32[208,128]{1,0:T(8,128)}, u32[]{:S(2)}) copy-start(f32[208,128]{1,0:T(8,128)} %constant.8.clone.seed_ref) | copy-start | bytes 319492
  29.4 0.7 copy-start.6
  30.1 23.9 %all-to-all-start.1 = ((f32[32,16,128]{2,1,0:T(8,128)}), f32[32,16,128]{2,1,0:T(8,128)S(1)}, u32[]{:S(2)}, u32[]{:S(2)}) async-start(f32[32,16,128]{2,1,0:T(8,128)} %bitcast.3), calls=%async_computation.1 | async-start | bytes 524288 | tf_op jit(solution)/shard_map/all_to_all | solution.py:384
  39.9 25.3 %collective-permute-start.2 = (f32[1160,128]{1,0:T(8,128)S(1)}, f32[1160,128]{1,0:T(8,128)S(1)}, u32[]{:S(2)}, u32[]{:S(2)}) collective-permute-start(f32[1160,128]{1,0:T(8,128)S(1)} %get-tuple-element.6.r_ref.up_ref), channel_id=1, source_target_pairs={{0,1},{1,2},{2,3},{3,4},{4,5},{5,6},{6,7},{7,8},{8,9},{9,10},{10,1... | collective-permute-start | bytes 1781768 | tf_op jit(solution)/shard_map/ppermute | solution.py:402
  44.2 22.6 %collective-permute-start.3 = (f32[1160,128]{1,0:T(8,128)S(1)}, f32[1160,128]{1,0:T(8,128)S(1)}, u32[]{:S(2)}, u32[]{:S(2)}) collective-permute-start(f32[1160,128]{1,0:T(8,128)S(1)} %get-tuple-element.9.down_ref), channel_id=1, source_target_pairs={{1,0},{2,1},{3,2},{4,3},{5,4},{6,5},{7,6},{8,7},{9,8},{10,9},{11,1... | collective-permute-start | bytes 1781768 | tf_op jit(solution)/shard_map/ppermute | solution.py:403
  54.1 12.7 %copy-start.2 = (bf16[2,240,256]{2,1,0:T(8,128)(2,1)S(1)}, bf16[2,240,256]{2,1,0:T(8,128)(2,1)}, u32[]{:S(2)}) copy-start(bf16[2,240,256]{2,1,0:T(8,128)(2,1)} %constant.6.clone.bh_ref) | copy-start | bytes 737284
  54.1 12.6 %copy-start.3 = (bf16[2,240,256]{2,1,0:T(8,128)(2,1)S(1)}, bf16[2,240,256]{2,1,0:T(8,128)(2,1)}, u32[]{:S(2)}) copy-start(bf16[2,240,256]{2,1,0:T(8,128)(2,1)} %constant.7.clone.bl_ref) | copy-start | bytes 737284
  54.1 12.6 %copy-start.7 = (f32[768,128]{1,0:T(8,128)S(1)}, f32[768,128]{1,0:T(8,128)}, u32[]{:S(2)}) copy-start(f32[768,128]{1,0:T(8,128)} %copy-done.6) | copy-start | bytes 1179652
where the time goes:
time: 75.9 us; the launch traced here: 75.5 us
  starting transfers between devices  40.6 us (53%)
  Pallas kernels  15.2 us (20%)
  waiting for transfers between devices  14.9 us (20%)
  local copies, waits for them, and re-layouts  3.43 us (5%)
  between operations  1.41 us (2%)
    all_to_all x2, starting transfers between devices, exchange(): lax.all_to_all(block, 'wa', split_axis=0, concat_axis=0, tiled=True)  20 us
    pallas_call x5, Pallas kernels, run(): pl.pallas_call(kernel, out_shape=outs, in_specs=specs, out_specs=jax.tree...  15.2 us
    ppermute x1, waiting for transfers between devices, shards(): from_low = lax.ppermute(to_up, 'gz', up)  9.3 us
    ppermute x1, starting transfers between devices, shards(): from_high = lax.ppermute(to_down, 'gz', down)  9.23 us
    ppermute x1, starting transfers between devices, shards(): after = lax.ppermute(scalar[:, 0:2, :].reshape(8, 1024), 'wa', down)  5.04 us
    ppermute x1, starting transfers between devices, shards(): from_low = lax.ppermute(to_up, 'gz', up)  4.28 us
    unnamed x16, local copies, waits for them, and re-layouts  3.36 us
    all_to_all x2, waiting for transfers between devices, exchange(): lax.all_to_all(block, 'wa', split_axis=0, concat_axis=0, tiled=True)  2.42 us
  transfers between devices with their start and end apart: 6, of which 5 were waited for; matrix products, arithmetic and copies ran while one was open for 0% of the time, Pallas kernels for 2%

commit v1 on v0

--- a/solution.py
+++ b/solution.py
@@ -86,13 +86,35 @@
     return lax.broadcasted_iota(jnp.int32, shape, len(shape) - 1)
 
 
+def cos_sin(steps):
+    centred = jnp.where(steps >= N // 2, steps - N, steps)
+    quarter = centred.astype(F32) * (math.pi / (2 * N))
+    square = quarter * quarter
+    sin = cos = jnp.zeros_like(square)
+    for i in range(5, -1, -1):
+        sin = sin * square + (-1) ** i / math.factorial(2 * i + 1)
+        cos = cos * square + (-1) ** i / math.factorial(2 * i)
+    sin = sin * quarter
+    for _ in range(2):
+        sin, cos = 2.0 * sin * cos, 1.0 - 2.0 * sin * sin
+    return cos, sin
+
+
+def make_seeds(seed_ref):
+    for first, count, scale in ((0, 96, 8), (192, 8, 1)):
+        row = lax.broadcasted_iota(jnp.int32, (count, 128), 0)
+        cos, sin = cos_sin(lax.rem(scale * row * lanes_of((count, 128)), N))
+        seed_ref[first : first + count, :] = cos
+        seed_ref[first + count : first + 2 * count, :] = sin
+
+
 def make_table(seed_ref, fh_ref, fl_ref, blocks=(0, 1, 2, 3, 4, 5)):
     near_cos, near_sin = seed_ref[192:200, :], seed_ref[200:208, :]
     sublane = lax.broadcasted_iota(jnp.int32, (8, 128), 0)
     turns = []
     for phase in range(3):
         turns.append([])
-        for b in range(6):
+        for b in range(3):
             sixth = lax.rem(b * (2 * phase + sublane), 6)
             cos, sin = jnp.ones((8, 128), F32), jnp.zeros((8, 128), F32)
             for i in range(1, 6):
@@ -100,32 +122,40 @@
                 cos = jnp.where(sixth == i, round(math.cos(angle), 6), cos)
                 sin = jnp.where(sixth == i, 0.0 if i == 3 else math.sin(angle), sin)
             turns[-1].append((cos, sin))
+    parity = jnp.bitwise_and(lax.broadcasted_iota(jnp.int32, (16, 128), 0), 1)
+    sign = (1 - 2 * parity).astype(F32).astype(BF16)
 
     def six(step, carry):
         for pair in range(3):
-            parts = []
+            parts = ([], [], [])
             for i in (2 * pair, 2 * pair + 1):
                 m = 6 * step + i
                 far_cos, far_sin = seed_ref[pl.ds(m, 1), :], seed_ref[pl.ds(96 + m, 1), :]
                 cos = far_cos * near_cos - far_sin * near_sin
                 sin = far_sin * near_cos + far_cos * near_sin
                 plus, minus = cos + sin, cos - sin
-                tiles = []
-                for b in blocks:
+                parts[0].append(plus)
+                for b in (1, 2):
                     turn_cos, turn_sin = turns[i % 3][b]
-                    tiles.append(turn_cos * plus + turn_sin * minus if b else plus)
-                parts.append(jnp.concatenate(tiles, axis=1))
-            high, low = split(jnp.concatenate(parts, axis=0))
+                    parts[b].append(turn_cos * plus + turn_sin * minus)
+            halves = [split(jnp.concatenate(p, axis=0)) for p in parts]
             row = pl.multiple_of(48 * step + 16 * pair, 16)
-            fh_ref[pl.ds(row, 16), :] = high
-            fl_ref[pl.ds(row, 16), :] = low
+            for place, b in enumerate(blocks):
+                for ref, half in zip((fh_ref, fl_ref), halves[b % 3]):
+                    ref[pl.ds(row, 16), 128 * place : 128 * place + 128] = (
+                        half if b < 3 else half * sign
+                    )
         return carry
 
-    lax.fori_loop(0, 16, six, 0)
-
-
-def synth_y_kernel(m_ref, seed_ref, out_ref, fh_ref, fl_ref):
+    lax.fori_loop(0, 16, six, 0, unroll=4)
+
+
+def synth_y_kernel(m_hbm, out_ref, fh_ref, fl_ref, seed_ref, m_ref, sem):
+    modes_copy = pltpu.make_async_copy(m_hbm, m_ref, sem)
+    modes_copy.start()
+    make_seeds(seed_ref)
     make_table(seed_ref, fh_ref, fl_ref)
+    modes_copy.wait()
     mh, ml = split(m_ref[...])
     both = jnp.concatenate([mh, ml], axis=0)
     stacked = mm(both[:, :HALF], fh_ref[0:HALF, :]) + mm(both[:, HALF:], fh_ref[512:, :])
@@ -166,14 +196,13 @@
             ref[row + 36 : row + 40, :] = jnp.zeros((4, 128), F32)
 
 
-def spectral_kernel(r_ref, seed_ref, spaced_ref, out_ref, fh_ref, fl_ref):
+def spectral_kernel(r_ref, seed_ref, out_ref, fh_ref, fl_ref):
     make_table(seed_ref, fh_ref, fl_ref)
     rh, rl = split(r_ref[0:BASE, :])
     both = jnp.concatenate([rh, rl], axis=1)
     o = mm(fh_ref[:, 0:HALF], both[0:HALF]) + mm(fh_ref[:, 512:], both[HALF:])
     spaced = o[:, :128] + o[:, 128:]
     spaced = spaced + mm(fl_ref[:, 0:HALF], rh[0:HALF]) + mm(fl_ref[:, 512:], rh[HALF:])
-    spaced_ref[...] = spaced
     swapped = pltpu.roll(spaced, 64, 1)
     products = jnp.where(
         lanes_of((N, 128)) < 64,
@@ -216,20 +245,18 @@
     out_ref[...] = (o * (1.0 / N)).astype(BF16)
 
 
-def flux(g, gg, h, hh):
-    return (h - g) * (gg + hh)
+def flux(g, gg, h):
+    return (h - g) * (gg + h * h)
 
 
 def fine_kernel(
     shift_ref,
-    spaced_ref,
     up_ref,
     down_ref,
     low_ref,
     high_ref,
     seed_ref,
-    bh_ref,
-    bl_ref,
+    b_ref,
     out_ref,
     fh_ref,
     fl_ref,
@@ -243,9 +270,10 @@
     left = lanes_of((BASE, 128)) < 64
     first = jnp.where(left, below, pltpu.roll(above, 64, 1))
     second = jnp.where(left, pltpu.roll(below, 64, 1), above)
-    rh, rl = split(jnp.concatenate([first, second], axis=1))
+    rh, rl = split(jnp.concatenate([first, second, up_ref[0:BASE, :]], axis=1))
     halo = mm(fh_ref[...], rh) + mm(fh_ref[...], rl) + mm(fl_ref[...], rh)
-    for i, tile in enumerate((halo[:, :128], halo[:, 128:], spaced_ref[...])):
+    for i in range(3):
+        tile = halo[:, 128 * i : 128 * i + 128]
         x_ref[i, 0:N, :] = tile
         x_ref[i, N : N + 128, :] = tile[0:128]
 
@@ -282,7 +310,8 @@
         for c in range(2):
             mine = jnp.concatenate([lines[:, 128 * c : 128 * c + 128], lines[:, 256:]], axis=1)
             vh, vl = split(mine)
-            o = mm_nt(bh_ref[c], vh) + mm_nt(bl_ref[c], vh) + mm_nt(bh_ref[c], vl)
+            o = mm_nt(b_ref[c], vh)
+            o = o[:240] + o[240:] + mm_nt(b_ref[c, 0:240, :], vl)
             u_ref[c, 2 * pair] = o[:, :128]
             u_ref[c, 2 * pair + 1] = o[:, 128:]
 
@@ -291,8 +320,8 @@
 
     def around(centre, west, east):
         lane = lanes_of(centre.shape)
-        to_east = jnp.where(lane == 127, pltpu.roll(east, 127, 1), pltpu.roll(centre, 127, 1))
-        to_west = jnp.where(lane == 0, pltpu.roll(west, 1, 1), pltpu.roll(centre, 1, 1))
+        to_east = pltpu.roll(jnp.where(lane == 0, east, centre), 127, 1)
+        to_west = pltpu.roll(jnp.where(lane == 127, west, centre), 1, 1)
         return to_west, to_east
 
     def rate(load, planes, count, skip, use):
@@ -301,33 +330,29 @@
             east_t = lax.rem(t + 1, 8)
             first = planes[0]
             g = load(first, t, skip, count)
-            gg = 1.0 + g * g
+            gg = 2.0 + g * g
             below = load(first - 1, t, skip, count)
-            lower = flux(below, 1.0 + below * below, g, gg)
+            lower = -flux(g, gg, below)
             for p in planes:
                 above = load(p + 1, t, skip, count)
-                aa = 1.0 + above * above
-                upper = flux(g, gg, above, aa)
                 north = load(p, t, skip + 1, count)
                 south = load(p, t, skip - 1, count)
                 west, east = around(
                     g, load(p, west_t, skip, count), load(p, east_t, skip, count)
                 )
-                total = flux(g, gg, north, 1.0 + north * north) + flux(
-                    g, gg, south, 1.0 + south * south
-                )
-                total = total + flux(g, gg, east, 1.0 + east * east)
-                total = total + flux(g, gg, west, 1.0 + west * west)
+                row = (p - 1) * EXT + skip
+                total = u_ref[0, t, row : row + count, :] * (east - west)
+                total = total + u_ref[1, t, row : row + count, :] * (north - south)
+                total = total + flux(g, gg, north) + flux(g, gg, south)
+                total = total + flux(g, gg, east) + flux(g, gg, west)
+                square = above * above
+                upper = (above - g) * (gg + square)
                 total = total + upper - lower
-                row = (p - 1) * EXT + skip
-                along_x = u_ref[0, t, row : row + count, :]
-                along_y = u_ref[1, t, row : row + count, :]
-                wind = along_x * (east - west) + along_y * (north - south)
-                use(p, t, g, g + (0.01 * total - 0.1 * wind))
-                lower, g, gg = upper, above, aa
+                use(p, t, g, g + 0.01 * total)
+                lower, g, gg = upper, above, 2.0 + square
             return carry
 
-        lax.fori_loop(0, 8, one, 0)
+        lax.fori_loop(0, 8, one, 0, unroll=2)
 
     def load_scalar(p, t, skip, count):
         ref, plane = homes[p]
@@ -351,11 +376,12 @@
     rate(load_section, range(2, 6), 32, 2, keep_result)
 
 
-def call(kernel, outs, flops, limit, scratch=(), smem=0):
+def call(kernel, outs, flops, limit, scratch=(), smem=0, home=pltpu.VMEM):
     vmem = pl.BlockSpec(memory_space=pltpu.VMEM)
+    place = pl.BlockSpec(memory_space=home)
 
     def run(*args):
-        specs = [pl.BlockSpec(memory_space=pltpu.SMEM)] * smem + [vmem] * (len(args) - smem)
+        specs = [pl.BlockSpec(memory_space=pltpu.SMEM)] * smem + [place] * (len(args) - smem)
         size = sum(math.prod(a.shape) * a.dtype.itemsize for a in args)
         return pl.pallas_call(
             kernel,
@@ -371,7 +397,7 @@
 
 
 def shards(velocity_modes, scalar, nest_shift):
-    bh, bl = (jnp.asarray(a) for a in split_host(row_plane_matrix()))
+    stencil = jnp.asarray(np.concatenate(split_host(-10.0 * row_plane_matrix()), axis=1))
     of = jax.ShapeDtypeStruct
 
     def ring(axis):
@@ -387,7 +413,19 @@
     seeds = jnp.asarray(cas_seeds())
     full = (pltpu.VMEM((N, N), BF16),) * 2
     retained = (pltpu.VMEM((N, 512), BF16),) * 2
-    sent = call(synth_y_kernel, of((512, 128), F32), 10**9, 12, scratch=full)(modes, seeds)
+    sent = call(
+        synth_y_kernel,
+        of((512, 128), F32),
+        10**9,
+        60,
+        scratch=full
+        + (
+            pltpu.VMEM((208, 128), F32),
+            pltpu.VMEM((64, 512), F32),
+            pltpu.SemaphoreType.DMA(()),
+        ),
+        home=pltpu.HBM,
+    )(modes)
     received = exchange(sent)
 
     up, down = ring("wa")
@@ -402,9 +440,7 @@
     from_low = lax.ppermute(to_up, "gz", up)
     from_high = lax.ppermute(to_down, "gz", down)
 
-    spaced, half = call(
-        spectral_kernel, (of((N, 128), F32), of((512, 128), F32)), 10**9, 12, scratch=full
-    )(to_up, seeds)
+    half = call(spectral_kernel, of((512, 128), F32), 10**9, 12, scratch=full)(to_up, seeds)
     returned = exchange(half)
 
     scalar_next = call(
@@ -419,7 +455,7 @@
             pltpu.VMEM((6 * 8 * EXT + 8, 128), F32),
         ),
         smem=1,
-    )(nest_shift, spaced, to_up, to_down, from_low, from_high, seeds, bh, bl)
+    )(nest_shift, to_up, to_down, from_low, from_high, seeds, stencil)
 
     stress = call(
         analysis_y_kernel, of((64, 512), BF16), 10**9, 8, scratch=retained

time: 75.9 us -> 71.8 us (0.946)
  local copies, waits for them, and re-layouts: 3.43 us -> 0.89 us
  Pallas kernels: 15.2 us -> 13.7 us
    unnamed x16 -> x6, local copies, waits for them, and re-layouts: 3.36 us -> 0.81 us
    pallas_call x5, Pallas kernels: 15.2 us -> 13.7 us  [run(): pl.pallas_call(kernel, out_shape=outs, in_specs=specs, out_specs=jax.tree...]
where the time goes in v1:
time: 71.8 us; the launch traced here: 71.4 us
  starting transfers between devices  40.6 us (57%)
  waiting for transfers between devices  14.9 us (21%)
  Pallas kernels  13.7 us (19%)
  between operations  1.4 us (2%)
  local copies, waits for them, and re-layouts  0.89 us (1%)
    all_to_all x2, starting transfers between devices, exchange(): lax.all_to_all(block, 'wa', split_axis=0, concat_axis=0, tiled=True)  20 us
    pallas_call x5, Pallas kernels, run(): pl.pallas_call(kernel, out_shape=outs, in_specs=specs, out_specs=jax.tree...  13.7 us
    ppermute x1, waiting for transfers between devices, shards(): from_low = lax.ppermute(to_up, 'gz', up)  9.36 us
    ppermute x1, starting transfers between devices, shards(): from_high = lax.ppermute(to_down, 'gz', down)  9.22 us
    ppermute x1, starting transfers between devices, shards(): after = lax.ppermute(scalar[:, 0:2, :].reshape(8, 1024), 'wa', down)  5.04 us
    ppermute x1, starting transfers between devices, shards(): from_low = lax.ppermute(to_up, 'gz', up)  4.27 us
    all_to_all x2, waiting for transfers between devices, exchange(): lax.all_to_all(block, 'wa', split_axis=0, concat_axis=0, tiled=True)  2.42 us
    ppermute x1, starting transfers between devices, shards(): before = lax.ppermute(scalar[:, 30:32, :].reshape(8, 1024), 'wa', up)  2.02 us
  transfers between devices with their start and end apart: 6, of which 5 were waited for; matrix products, arithmetic and copies ran while one was open for 0% of the time, Pallas kernels for 2%

profile of v1, /device:TPU:12, one launch (start us, length us, event | category | flops | bytes accessed | tf_op | source)
XLA Modules:
  0.0 71.4 jit_solution(3456956526982205364)
XLA Ops:
  0.6 2.3 %shard_map.68 = f32[512,128]{1,0:T(8,128)} custom-call(f32[64,512]{1,0:T(8,128)} %bitcast.9), custom_call_target="tpu_custom_call" | custom-call | flops 1000000000 | bytes 131072 | tf_op jit(solution)/shard_map/pallas_call | solution.py:386
  2.9 0.0 copy-start
  2.9 10.3 %all-to-all-start = ((f32[32,16,128]{2,1,0:T(8,128)}), f32[32,16,128]{2,1,0:T(8,128)S(1)}, u32[]{:S(2)}, u32[]{:S(2)}) async-start(f32[32,16,128]{2,1,0:T(8,128)} %bitcast.8), calls=%async_computation | async-start | bytes 524288 | tf_op jit(solution)/shard_map/all_to_all | solution.py:410
  13.2 0.0 copy-done
  13.3 2.0 %collective-permute-start = (f32[8,1024]{1,0:T(8,128)S(1)}, f32[8,1024]{1,0:T(8,128)S(1)}, u32[]{:S(2)}, u32[]{:S(2)}) collective-permute-start(f32[8,1024]{1,0:T(8,128)S(1)} %reshape.31), channel_id=1, source_target_pairs={{0,16},{16,32},{32,48},{48,64},{64,80},{80,96},{96,112},{112,128},... | collective-permute-start | bytes 98312 | tf_op jit(solution)/shard_map/ppermute | solution.py:432
  15.3 5.0 %collective-permute-start.1 = (f32[8,1024]{1,0:T(8,128)S(1)}, f32[8,1024]{1,0:T(8,128)S(1)}, u32[]{:S(2)}, u32[]{:S(2)}) collective-permute-start(f32[8,1024]{1,0:T(8,128)S(1)} %reshape.32), channel_id=1, source_target_pairs={{16,0},{32,16},{48,32},{64,48},{80,64},{96,80},{112,96},{128,112},... | collective-permute-start | bytes 98312 | tf_op jit(solution)/shard_map/ppermute | solution.py:433
  20.4 0.1 collective-permute-done.before_ref
  20.5 1.5 %collective-permute-done.1.after_ref = f32[8,1024]{1,0:T(8,128)S(1)} collective-permute-done((f32[8,1024]{1,0:T(8,128)S(1)}, f32[8,1024]{1,0:T(8,128)S(1)}, u32[]{:S(2)}, u32[]{:S(2)}) %collective-permute-start.1) | collective-permute-done | bytes 32800 | tf_op jit(solution)/shard_map/ppermute | solution.py:433
  22.0 2.4 %all-to-all-done = f32[32,16,128]{2,1,0:T(8,128)S(1)} async-done(((f32[32,16,128]{2,1,0:T(8,128)}), f32[32,16,128]{2,1,0:T(8,128)S(1)}, u32[]{:S(2)}, u32[]{:S(2)}) %all-to-all-start) | async-done | bytes 262176 | tf_op jit(solution)/shard_map/all_to_all | solution.py:410
  24.4 0.0 copy-start.2
  24.4 0.1 shard_map.69
  24.5 0.8 %copy-done.2 = f32[208,128]{1,0:T(8,128)S(1)} copy-done((f32[208,128]{1,0:T(8,128)S(1)}, f32[208,128]{1,0:T(8,128)}, u32[]{:S(2)}) %copy-start.2) | copy-done | bytes 106520
  25.3 2.3 %shard_map.70 = f32[512,128]{1,0:T(8,128)} custom-call(f32[1160,128]{1,0:T(8,128)S(1)} %get-tuple-element.4.r_ref.up_ref, f32[208,128]{1,0:T(8,128)S(1)} %copy-done.2), custom_call_target="tpu_custom_call" | custom-call | flops 1000000000 | bytes 700416 | tf_op jit(solution)/shard_map/pallas_call | solution.py:386
  27.6 9.7 %all-to-all-start.1 = ((f32[32,16,128]{2,1,0:T(8,128)}), f32[32,16,128]{2,1,0:T(8,128)S(1)}, u32[]{:S(2)}, u32[]{:S(2)}) async-start(f32[32,16,128]{2,1,0:T(8,128)} %bitcast.3), calls=%async_computation.1 | async-start | bytes 524288 | tf_op jit(solution)/shard_map/all_to_all | solution.py:410
  37.4 4.3 %collective-permute-start.2 = (f32[1160,128]{1,0:T(8,128)S(1)}, f32[1160,128]{1,0:T(8,128)S(1)}, u32[]{:S(2)}, u32[]{:S(2)}) collective-permute-start(f32[1160,128]{1,0:T(8,128)S(1)} %get-tuple-element.4.r_ref.up_ref), channel_id=1, source_target_pairs={{0,1},{1,2},{2,3},{3,4},{4,5},{5,6},{6,7},{7,8},{8,9},{9,10},{10,1... | collective-permute-start | bytes 1781768 | tf_op jit(solution)/shard_map/ppermute | solution.py:440
  41.7 9.2 %collective-permute-start.3 = (f32[1160,128]{1,0:T(8,128)S(1)}, f32[1160,128]{1,0:T(8,128)S(1)}, u32[]{:S(2)}, u32[]{:S(2)}) collective-permute-start(f32[1160,128]{1,0:T(8,128)S(1)} %get-tuple-element.5.down_ref), channel_id=1, source_target_pairs={{1,0},{2,1},{3,2},{4,3},{5,4},{6,5},{7,6},{8,7},{9,8},{10,9},{11,1... | collective-permute-start | bytes 1781768 | tf_op jit(solution)/shard_map/ppermute | solution.py:441
  51.5 0.0 all-to-all-done.1
  51.5 0.0 copy-start.1
  51.6 1.7 %shard_map.71 = bf16[64,512]{1,0:T(8,128)(2,1)} custom-call(f32[512,128]{1,0:T(8,128)S(1)} %bitcast.7, f32[208,128]{1,0:T(8,128)S(1)} %copy-done.2), custom_call_target="tpu_custom_call" | custom-call | flops 1000000000 | bytes 368640 | tf_op jit(solution)/shard_map/pallas_call | solution.py:386
  53.3 9.4 %collective-permute-done.2.low_ref = f32[1160,128]{1,0:T(8,128)S(1)} collective-permute-done((f32[1160,128]{1,0:T(8,128)S(1)}, f32[1160,128]{1,0:T(8,128)S(1)}, u32[]{:S(2)}, u32[]{:S(2)}) %collective-permute-start.2) | collective-permute-done | bytes 593952 | tf_op jit(solution)/shard_map/ppermute | solution.py:440
  62.6 1.6 %collective-permute-done.3.high_ref = f32[1160,128]{1,0:T(8,128)S(1)} collective-permute-done((f32[1160,128]{1,0:T(8,128)S(1)}, f32[1160,128]{1,0:T(8,128)S(1)}, u32[]{:S(2)}, u32[]{:S(2)}) %collective-permute-start.3) | collective-permute-done | bytes 593952 | tf_op jit(solution)/shard_map/ppermute | solution.py:441
  64.2 0.0 copy-done.1
  64.2 7.2 %shard_map.72 = f32[4,32,1024]{2,1,0:T(8,128)} custom-call(s32[1]{0:T(128)S(6)} %copy.7.shift_ref, f32[1160,128]{1,0:T(8,128)S(1)} %get-tuple-element.4.r_ref.up_ref, f32[1160,128]{1,0:T(8,128)S(1)} %get-tuple-element.5.down_ref, f32[1160,128]{1,0:T(8,128)S(1)} %collective-permute-done.2.low_ref, f32[1160,128]{1,0:T(8,128)S(1)} %collective-permute-done.3.high_ref, ...), custom_call_target="tpu_custom_call" | custom-call | flops 2000000000 | bytes 2973700 | tf_op jit(solution)/shard_map/pallas_call | solution.py:386
  (3 shorter events, 0.1 us)
Async XLA Ops:
  2.9 10.3 %copy-start = (f32[4,32,1024]{2,1,0:T(8,128)S(1)}, f32[4,32,1024]{2,1,0:T(8,128)}, u32[]{:S(2)}) copy-start(f32[4,32,1024]{2,1,0:T(8,128)} %g_ref.1) | copy-start | bytes 1572868
  2.9 21.4 %all-to-all-start = ((f32[32,16,128]{2,1,0:T(8,128)}), f32[32,16,128]{2,1,0:T(8,128)S(1)}, u32[]{:S(2)}, u32[]{:S(2)}) async-start(f32[32,16,128]{2,1,0:T(8,128)} %bitcast.8), calls=%async_computation | async-start | bytes 524288 | tf_op jit(solution)/shard_map/all_to_all | solution.py:410
  13.3 7.2 %collective-permute-start = (f32[8,1024]{1,0:T(8,128)S(1)}, f32[8,1024]{1,0:T(8,128)S(1)}, u32[]{:S(2)}, u32[]{:S(2)}) collective-permute-start(f32[8,1024]{1,0:T(8,128)S(1)} %reshape.31), channel_id=1, source_target_pairs={{0,16},{16,32},{32,48},{48,64},{64,80},{80,96},{96,112},{112,128},... | collective-permute-start | bytes 98312 | tf_op jit(solution)/shard_map/ppermute | solution.py:432
  15.3 6.6 %collective-permute-start.1 = (f32[8,1024]{1,0:T(8,128)S(1)}, f32[8,1024]{1,0:T(8,128)S(1)}, u32[]{:S(2)}, u32[]{:S(2)}) collective-permute-start(f32[8,1024]{1,0:T(8,128)S(1)} %reshape.32), channel_id=1, source_target_pairs={{16,0},{32,16},{48,32},{64,48},{80,64},{96,80},{112,96},{128,112},... | collective-permute-start | bytes 98312 | tf_op jit(solution)/shard_map/ppermute | solution.py:433
  24.4 0.9 %copy-start.2 = (f32[208,128]{1,0:T(8,128)S(1)}, f32[208,128]{1,0:T(8,128)}, u32[]{:S(2)}) copy-start(f32[208,128]{1,0:T(8,128)} %constant.5.clone.seed_ref) | copy-start | bytes 319492
  27.6 23.9 %all-to-all-start.1 = ((f32[32,16,128]{2,1,0:T(8,128)}), f32[32,16,128]{2,1,0:T(8,128)S(1)}, u32[]{:S(2)}, u32[]{:S(2)}) async-start(f32[32,16,128]{2,1,0:T(8,128)} %bitcast.3), calls=%async_computation.1 | async-start | bytes 524288 | tf_op jit(solution)/shard_map/all_to_all | solution.py:410
  37.4 25.3 %collective-permute-start.2 = (f32[1160,128]{1,0:T(8,128)S(1)}, f32[1160,128]{1,0:T(8,128)S(1)}, u32[]{:S(2)}, u32[]{:S(2)}) collective-permute-start(f32[1160,128]{1,0:T(8,128)S(1)} %get-tuple-element.4.r_ref.up_ref), channel_id=1, source_target_pairs={{0,1},{1,2},{2,3},{3,4},{4,5},{5,6},{6,7},{7,8},{8,9},{9,10},{10,1... | collective-permute-start | bytes 1781768 | tf_op jit(solution)/shard_map/ppermute | solution.py:440
  41.7 22.5 %collective-permute-start.3 = (f32[1160,128]{1,0:T(8,128)S(1)}, f32[1160,128]{1,0:T(8,128)S(1)}, u32[]{:S(2)}, u32[]{:S(2)}) collective-permute-start(f32[1160,128]{1,0:T(8,128)S(1)} %get-tuple-element.5.down_ref), channel_id=1, source_target_pairs={{1,0},{2,1},{3,2},{4,3},{5,4},{6,5},{7,6},{8,7},{9,8},{10,9},{11,1... | collective-permute-start | bytes 1781768 | tf_op jit(solution)/shard_map/ppermute | solution.py:441
  51.5 12.7 %copy-start.1 = (bf16[2,480,256]{2,1,0:T(8,128)(2,1)S(1)}, bf16[2,480,256]{2,1,0:T(8,128)(2,1)}, u32[]{:S(2)}) copy-start(bf16[2,480,256]{2,1,0:T(8,128)(2,1)} %constant.4.clone.b_ref) | copy-start | bytes 1474564

commit v2 on v1

--- a/solution.py
+++ b/solution.py
@@ -17,7 +17,6 @@
 OWN = 24
 ROWS = 32
 EXT = 40
-RETAINED = (0, 1, 4, 5)
 BASE = 512
 PAYLOAD = BASE + 2 * 8 * EXT + 8
 
@@ -108,7 +107,22 @@
         seed_ref[first + count : first + 2 * count, :] = sin
 
 
-def make_table(seed_ref, fh_ref, fl_ref, blocks=(0, 1, 2, 3, 4, 5)):
+def sign_of(shape, dimension):
+    return (1 - 2 * jnp.bitwise_and(lax.broadcasted_iota(jnp.int32, shape, dimension), 1)).astype(F32)
+
+
+def three(fh, fl, high, low):
+    return mm(fh, high) + mm(fh, low) + mm(fl, high)
+
+
+def synth_x(fh_ref, fl_ref, lines):
+    high, low = split(jnp.concatenate([lines, lines * sign_of(lines.shape, 0)], axis=1))
+    plus = three(fh_ref[:, :HALF], fl_ref[:, :HALF], high[:HALF], low[:HALF])
+    minus = three(fh_ref[:, 128:], fl_ref[:, 128:], high[HALF:], low[HALF:])
+    return plus + sign_of(minus.shape, 0) * minus
+
+
+def make_table(seed_ref, fh_ref, fl_ref):
     near_cos, near_sin = seed_ref[192:200, :], seed_ref[200:208, :]
     sublane = lax.broadcasted_iota(jnp.int32, (8, 128), 0)
     turns = []
@@ -122,8 +136,6 @@
                 cos = jnp.where(sixth == i, round(math.cos(angle), 6), cos)
                 sin = jnp.where(sixth == i, 0.0 if i == 3 else math.sin(angle), sin)
             turns[-1].append((cos, sin))
-    parity = jnp.bitwise_and(lax.broadcasted_iota(jnp.int32, (16, 128), 0), 1)
-    sign = (1 - 2 * parity).astype(F32).astype(BF16)
 
     def six(step, carry):
         for pair in range(3):
@@ -140,14 +152,12 @@
                     parts[b].append(turn_cos * plus + turn_sin * minus)
             halves = [split(jnp.concatenate(p, axis=0)) for p in parts]
             row = pl.multiple_of(48 * step + 16 * pair, 16)
-            for place, b in enumerate(blocks):
-                for ref, half in zip((fh_ref, fl_ref), halves[b % 3]):
-                    ref[pl.ds(row, 16), 128 * place : 128 * place + 128] = (
-                        half if b < 3 else half * sign
-                    )
+            for b in range(3):
+                for ref, half in zip((fh_ref, fl_ref), halves[b]):
+                    ref[pl.ds(row, 16), 128 * b : 128 * b + 128] = half
         return carry
 
-    lax.fori_loop(0, 16, six, 0, unroll=4)
+    lax.fori_loop(0, 8, six, 0, unroll=4)
 
 
 def synth_y_kernel(m_hbm, out_ref, fh_ref, fl_ref, seed_ref, m_ref, sem):
@@ -156,11 +166,18 @@
     make_seeds(seed_ref)
     make_table(seed_ref, fh_ref, fl_ref)
     modes_copy.wait()
-    mh, ml = split(m_ref[...])
-    both = jnp.concatenate([mh, ml], axis=0)
-    stacked = mm(both[:, :HALF], fh_ref[0:HALF, :]) + mm(both[:, HALF:], fh_ref[512:, :])
-    lines = stacked[:64] + stacked[64:]
-    lines = lines + mm(mh[:, :HALF], fl_ref[0:HALF, :]) + mm(mh[:, HALF:], fl_ref[512:, :])
+    modes = m_ref[...]
+    mh, ml = split(modes)
+    nh, nl = split(modes * sign_of(modes.shape, 1))
+    both = jnp.concatenate([mh, ml, nh, nl], axis=0)
+    high = jnp.concatenate([mh, nh], axis=0)
+    o = mm(both[:, HALF:], fh_ref[128:, :])
+    o = mm(both[:, :HALF], fh_ref[:HALF, :]) + sign_of(o.shape, 1) * o
+    p = mm(high[:, HALF:], fl_ref[128:, :])
+    p = mm(high[:, :HALF], fl_ref[:HALF, :]) + sign_of(p.shape, 1) * p
+    first = o[0:64] + o[64:128] + p[0:64]
+    second = o[128:192] + o[192:256] + p[64:128]
+    lines = jnp.concatenate([first, second], axis=1)
     tiles = [lines[:, 128 * t : 128 * t + 128] for t in range(6)]
     lane = lanes_of((64, 128))
     group = lanes_of((16, 128)) // 32
@@ -198,28 +215,27 @@
 
 def spectral_kernel(r_ref, seed_ref, out_ref, fh_ref, fl_ref):
     make_table(seed_ref, fh_ref, fl_ref)
-    rh, rl = split(r_ref[0:BASE, :])
-    both = jnp.concatenate([rh, rl], axis=1)
-    o = mm(fh_ref[:, 0:HALF], both[0:HALF]) + mm(fh_ref[:, 512:], both[HALF:])
-    spaced = o[:, :128] + o[:, 128:]
-    spaced = spaced + mm(fl_ref[:, 0:HALF], rh[0:HALF]) + mm(fl_ref[:, 512:], rh[HALF:])
-    swapped = pltpu.roll(spaced, 64, 1)
-    products = jnp.where(
-        lanes_of((N, 128)) < 64,
-        spaced * spaced - swapped * swapped,
-        spaced * swapped,
-    )
-    ph, plo = split(products)
-    both = jnp.concatenate([ph, plo], axis=1)
-    for first, row in ((0, 0), (512, HALF)):
-        o = mm(fh_ref[first : first + HALF, :], both)
-        out_ref[row : row + HALF, :] = (
-            o[:, :128] + o[:, 128:] + mm(fl_ref[first : first + HALF, :], ph)
+    spaced = synth_x(fh_ref, fl_ref, r_ref[0:BASE, :])
+    halves = []
+    for half in (spaced[:, :128], spaced[:, 128:]):
+        swapped = pltpu.roll(half, 64, 1)
+        halves.append(
+            jnp.where(
+                lanes_of(half.shape) < 64, half * half - swapped * swapped, half * swapped
+            )
         )
+    products = jnp.concatenate(halves, axis=1)
+    for first, row in ((0, 0), (128, HALF)):
+        if row:
+            products = products * sign_of(products.shape, 0)
+        high, low = split(products)
+        rows = slice(first, first + HALF)
+        o = three(fh_ref[rows, :], fl_ref[rows, :], high, low)
+        out_ref[row : row + HALF, :] = o[:, :128] + sign_of((HALF, 128), 0) * o[:, 128:]
 
 
 def analysis_y_kernel(r_ref, seed_ref, out_ref, fh_ref, fl_ref):
-    make_table(seed_ref, fh_ref, fl_ref, RETAINED)
+    make_table(seed_ref, fh_ref, fl_ref)
     lane = lanes_of((16, 128))
     columns = []
     for t in range(6):
@@ -238,11 +254,17 @@
             rows.append(tile)
         columns.append(jnp.concatenate(rows, axis=0))
     lines = jnp.concatenate(columns, axis=1)
-    ah, al = split(lines)
-    both = jnp.concatenate([ah, al], axis=0)
-    o = mm(both, fh_ref[...])
-    o = o[:64] + o[64:] + mm(ah, fl_ref[...])
-    out_ref[...] = (o * (1.0 / N)).astype(BF16)
+    for first, column in ((0, 0), (128, HALF)):
+        if column:
+            lines = lines * sign_of(lines.shape, 1)
+        high, low = split(lines)
+        rows = [part[:, 384 * i : 384 * i + 384] for i in range(2) for part in (high, low)]
+        o = mm(jnp.concatenate(rows, axis=0), fh_ref[:, first : first + HALF])
+        p = mm(jnp.concatenate(rows[::2], axis=0), fl_ref[:, first : first + HALF])
+        near = o[0:64] + o[64:128] + p[0:64]
+        far = o[128:192] + o[192:256] + p[64:128]
+        total = near + sign_of(far.shape, 1) * far
+        out_ref[:, column : column + HALF] = (total * (1.0 / N)).astype(BF16)
 
 
 def flux(g, gg, h):
@@ -264,18 +286,17 @@
     u_ref,
     s_ref,
 ):
-    make_table(seed_ref, fh_ref, fl_ref, RETAINED)
+    make_table(seed_ref, fh_ref, fl_ref)
     below = low_ref[0:BASE, :]
     above = high_ref[0:BASE, :]
     left = lanes_of((BASE, 128)) < 64
     first = jnp.where(left, below, pltpu.roll(above, 64, 1))
     second = jnp.where(left, pltpu.roll(below, 64, 1), above)
-    rh, rl = split(jnp.concatenate([first, second, up_ref[0:BASE, :]], axis=1))
-    halo = mm(fh_ref[...], rh) + mm(fh_ref[...], rl) + mm(fl_ref[...], rh)
-    for i in range(3):
-        tile = halo[:, 128 * i : 128 * i + 128]
-        x_ref[i, 0:N, :] = tile
-        x_ref[i, N : N + 128, :] = tile[0:128]
+    for i, lines in enumerate((first, second, up_ref[0:BASE, :])):
+        points = synth_x(fh_ref, fl_ref, lines)
+        x_ref[i, 0:384, :] = points[:, :128]
+        x_ref[i, 384:N, :] = points[:, 128:]
+        x_ref[i, N : N + 128, :] = points[0:128, :128]
 
     shift = shift_ref[0]
     base = lax.shift_right_arithmetic(3 * (1 + 2 * shift), 3) - 1
@@ -411,14 +432,13 @@
 
     modes = velocity_modes.reshape(64, 512)
     seeds = jnp.asarray(cas_seeds())
-    full = (pltpu.VMEM((N, N), BF16),) * 2
-    retained = (pltpu.VMEM((N, 512), BF16),) * 2
+    table = (pltpu.VMEM((N // 2, N // 2), BF16),) * 2
     sent = call(
         synth_y_kernel,
         of((512, 128), F32),
         10**9,
         60,
-        scratch=full
+        scratch=table
         + (
             pltpu.VMEM((208, 128), F32),
             pltpu.VMEM((64, 512), F32),
@@ -440,7 +460,7 @@
     from_low = lax.ppermute(to_up, "gz", up)
     from_high = lax.ppermute(to_down, "gz", down)
 
-    half = call(spectral_kernel, of((512, 128), F32), 10**9, 12, scratch=full)(to_up, seeds)
+    half = call(spectral_kernel, of((512, 128), F32), 10**9, 12, scratch=table)(to_up, seeds)
     returned = exchange(half)
 
     scalar_next = call(
@@ -448,7 +468,7 @@
         of((4, 32, 1024), F32),
         2 * 10**9,
         24,
-        scratch=retained
+        scratch=table
         + (
             pltpu.VMEM((3, N + 128, 128), F32),
             pltpu.VMEM((2, 8, 6 * EXT, 128), F32),
@@ -457,9 +477,7 @@
         smem=1,
     )(nest_shift, to_up, to_down, from_low, from_high, seeds, stencil)
 
-    stress = call(
-        analysis_y_kernel, of((64, 512), BF16), 10**9, 8, scratch=retained
-    )(returned, seeds)
+    stress = call(analysis_y_kernel, of((64, 512), BF16), 10**9, 8, scratch=table)(returned, seeds)
     return (stress.reshape(2, 2, 16, 512), scalar_next)
 
 

time: 71.8 us -> 71.1 us (level)
  Pallas kernels: 13.7 us -> 12.6 us
    pallas_call x5, Pallas kernels: 13.7 us -> 12.6 us  [run(): pl.pallas_call(kernel, out_shape=outs, in_specs=specs, out_specs=jax.tree...]
where the time goes in v2:
time: 71.1 us; the launch traced here: 70.7 us
  starting transfers between devices  40.6 us (57%)
  waiting for transfers between devices  15.2 us (21%)
  Pallas kernels  12.6 us (18%)
  between operations  1.4 us (2%)
  local copies, waits for them, and re-layouts  0.89 us (1%)
    all_to_all x2, starting transfers between devices, exchange(): lax.all_to_all(block, 'wa', split_axis=0, concat_axis=0, tiled=True)  20 us
    pallas_call x5, Pallas kernels, run(): pl.pallas_call(kernel, out_shape=outs, in_specs=specs, out_specs=jax.tree...  12.6 us
    ppermute x1, waiting for transfers between devices, shards(): from_low = lax.ppermute(to_up, 'gz', up)  9.65 us
    ppermute x1, starting transfers between devices, shards(): from_high = lax.ppermute(to_down, 'gz', down)  9.23 us
    ppermute x1, starting transfers between devices, shards(): after = lax.ppermute(scalar[:, 0:2, :].reshape(8, 1024), 'wa', down)  5.04 us
    ppermute x1, starting transfers between devices, shards(): from_low = lax.ppermute(to_up, 'gz', up)  4.28 us
    all_to_all x2, waiting for transfers between devices, exchange(): lax.all_to_all(block, 'wa', split_axis=0, concat_axis=0, tiled=True)  2.42 us
    ppermute x1, starting transfers between devices, shards(): before = lax.ppermute(scalar[:, 30:32, :].reshape(8, 1024), 'wa', up)  2.02 us
  transfers between devices with their start and end apart: 6, of which 5 were waited for; matrix products, arithmetic and copies ran while one was open for 0% of the time, Pallas kernels for 2%

profile of v2, /device:TPU:12, one launch (start us, length us, event | category | flops | bytes accessed | tf_op | source)
XLA Modules:
  0.0 70.7 jit_solution(14414447423216341205)
XLA Ops:
  0.6 2.3 %shard_map.68 = f32[512,128]{1,0:T(8,128)} custom-call(f32[64,512]{1,0:T(8,128)} %bitcast.9), custom_call_target="tpu_custom_call" | custom-call | flops 1000000000 | bytes 131072 | tf_op jit(solution)/shard_map/pallas_call | solution.py:407
  2.9 0.0 copy-start
  2.9 10.3 %all-to-all-start = ((f32[32,16,128]{2,1,0:T(8,128)}), f32[32,16,128]{2,1,0:T(8,128)S(1)}, u32[]{:S(2)}, u32[]{:S(2)}) async-start(f32[32,16,128]{2,1,0:T(8,128)} %bitcast.8), calls=%async_computation | async-start | bytes 524288 | tf_op jit(solution)/shard_map/all_to_all | solution.py:431
  13.2 0.0 copy-done
  13.3 2.0 %collective-permute-start = (f32[8,1024]{1,0:T(8,128)S(1)}, f32[8,1024]{1,0:T(8,128)S(1)}, u32[]{:S(2)}, u32[]{:S(2)}) collective-permute-start(f32[8,1024]{1,0:T(8,128)S(1)} %reshape.31), channel_id=1, source_target_pairs={{0,16},{16,32},{32,48},{48,64},{64,80},{80,96},{96,112},{112,128},... | collective-permute-start | bytes 98312 | tf_op jit(solution)/shard_map/ppermute | solution.py:452
  15.3 5.0 %collective-permute-start.1 = (f32[8,1024]{1,0:T(8,128)S(1)}, f32[8,1024]{1,0:T(8,128)S(1)}, u32[]{:S(2)}, u32[]{:S(2)}) collective-permute-start(f32[8,1024]{1,0:T(8,128)S(1)} %reshape.32), channel_id=1, source_target_pairs={{16,0},{32,16},{48,32},{64,48},{80,64},{96,80},{112,96},{128,112},... | collective-permute-start | bytes 98312 | tf_op jit(solution)/shard_map/ppermute | solution.py:453
  20.4 0.1 collective-permute-done.before_ref
  20.4 1.5 %collective-permute-done.1.after_ref = f32[8,1024]{1,0:T(8,128)S(1)} collective-permute-done((f32[8,1024]{1,0:T(8,128)S(1)}, f32[8,1024]{1,0:T(8,128)S(1)}, u32[]{:S(2)}, u32[]{:S(2)}) %collective-permute-start.1) | collective-permute-done | bytes 32800 | tf_op jit(solution)/shard_map/ppermute | solution.py:453
  21.9 2.4 %all-to-all-done = f32[32,16,128]{2,1,0:T(8,128)S(1)} async-done(((f32[32,16,128]{2,1,0:T(8,128)}), f32[32,16,128]{2,1,0:T(8,128)S(1)}, u32[]{:S(2)}, u32[]{:S(2)}) %all-to-all-start) | async-done | bytes 262176 | tf_op jit(solution)/shard_map/all_to_all | solution.py:431
  24.4 0.0 copy-start.2
  24.4 0.1 shard_map.69
  24.5 0.8 %copy-done.2 = f32[208,128]{1,0:T(8,128)S(1)} copy-done((f32[208,128]{1,0:T(8,128)S(1)}, f32[208,128]{1,0:T(8,128)}, u32[]{:S(2)}) %copy-start.2) | copy-done | bytes 106520
  25.3 2.1 %shard_map.70 = f32[512,128]{1,0:T(8,128)} custom-call(f32[1160,128]{1,0:T(8,128)S(1)} %get-tuple-element.4.r_ref.up_ref, f32[208,128]{1,0:T(8,128)S(1)} %copy-done.2), custom_call_target="tpu_custom_call" | custom-call | flops 1000000000 | bytes 700416 | tf_op jit(solution)/shard_map/pallas_call | solution.py:407
  27.4 9.7 %all-to-all-start.1 = ((f32[32,16,128]{2,1,0:T(8,128)}), f32[32,16,128]{2,1,0:T(8,128)S(1)}, u32[]{:S(2)}, u32[]{:S(2)}) async-start(f32[32,16,128]{2,1,0:T(8,128)} %bitcast.3), calls=%async_computation.1 | async-start | bytes 524288 | tf_op jit(solution)/shard_map/all_to_all | solution.py:431
  37.1 4.3 %collective-permute-start.2 = (f32[1160,128]{1,0:T(8,128)S(1)}, f32[1160,128]{1,0:T(8,128)S(1)}, u32[]{:S(2)}, u32[]{:S(2)}) collective-permute-start(f32[1160,128]{1,0:T(8,128)S(1)} %get-tuple-element.4.r_ref.up_ref), channel_id=1, source_target_pairs={{0,1},{1,2},{2,3},{3,4},{4,5},{5,6},{6,7},{7,8},{8,9},{9,10},{10,1... | collective-permute-start | bytes 1781768 | tf_op jit(solution)/shard_map/ppermute | solution.py:460
  41.4 9.2 %collective-permute-start.3 = (f32[1160,128]{1,0:T(8,128)S(1)}, f32[1160,128]{1,0:T(8,128)S(1)}, u32[]{:S(2)}, u32[]{:S(2)}) collective-permute-start(f32[1160,128]{1,0:T(8,128)S(1)} %get-tuple-element.5.down_ref), channel_id=1, source_target_pairs={{1,0},{2,1},{3,2},{4,3},{5,4},{6,5},{7,6},{8,7},{9,8},{10,9},{11,1... | collective-permute-start | bytes 1781768 | tf_op jit(solution)/shard_map/ppermute | solution.py:461
  51.3 0.0 all-to-all-done.1
  51.3 0.0 copy-start.1
  51.3 1.4 %shard_map.71 = bf16[64,512]{1,0:T(8,128)(2,1)} custom-call(f32[512,128]{1,0:T(8,128)S(1)} %bitcast.7, f32[208,128]{1,0:T(8,128)S(1)} %copy-done.2), custom_call_target="tpu_custom_call" | custom-call | flops 1000000000 | bytes 368640 | tf_op jit(solution)/shard_map/pallas_call | solution.py:407
  52.7 9.7 %collective-permute-done.2.low_ref = f32[1160,128]{1,0:T(8,128)S(1)} collective-permute-done((f32[1160,128]{1,0:T(8,128)S(1)}, f32[1160,128]{1,0:T(8,128)S(1)}, u32[]{:S(2)}, u32[]{:S(2)}) %collective-permute-start.2) | collective-permute-done | bytes 593952 | tf_op jit(solution)/shard_map/ppermute | solution.py:460
  62.4 1.6 %collective-permute-done.3.high_ref = f32[1160,128]{1,0:T(8,128)S(1)} collective-permute-done((f32[1160,128]{1,0:T(8,128)S(1)}, f32[1160,128]{1,0:T(8,128)S(1)}, u32[]{:S(2)}, u32[]{:S(2)}) %collective-permute-start.3) | collective-permute-done | bytes 593952 | tf_op jit(solution)/shard_map/ppermute | solution.py:461
  63.9 0.0 copy-done.1
  63.9 6.7 %shard_map.72 = f32[4,32,1024]{2,1,0:T(8,128)} custom-call(s32[1]{0:T(128)S(6)} %copy.7.shift_ref, f32[1160,128]{1,0:T(8,128)S(1)} %get-tuple-element.4.r_ref.up_ref, f32[1160,128]{1,0:T(8,128)S(1)} %get-tuple-element.5.down_ref, f32[1160,128]{1,0:T(8,128)S(1)} %collective-permute-done.2.low_ref, f32[1160,128]{1,0:T(8,128)S(1)} %collective-permute-done.3.high_ref, ...), custom_call_target="tpu_custom_call" | custom-call | flops 2000000000 | bytes 2973700 | tf_op jit(solution)/shard_map/pallas_call | solution.py:407
  (3 shorter events, 0.1 us)
Async XLA Ops:
  2.9 10.3 %copy-start = (f32[4,32,1024]{2,1,0:T(8,128)S(1)}, f32[4,32,1024]{2,1,0:T(8,128)}, u32[]{:S(2)}) copy-start(f32[4,32,1024]{2,1,0:T(8,128)} %g_ref.1) | copy-start | bytes 1572868
  2.9 21.4 %all-to-all-start = ((f32[32,16,128]{2,1,0:T(8,128)}), f32[32,16,128]{2,1,0:T(8,128)S(1)}, u32[]{:S(2)}, u32[]{:S(2)}) async-start(f32[32,16,128]{2,1,0:T(8,128)} %bitcast.8), calls=%async_computation | async-start | bytes 524288 | tf_op jit(solution)/shard_map/all_to_all | solution.py:431
  13.3 7.2 %collective-permute-start = (f32[8,1024]{1,0:T(8,128)S(1)}, f32[8,1024]{1,0:T(8,128)S(1)}, u32[]{:S(2)}, u32[]{:S(2)}) collective-permute-start(f32[8,1024]{1,0:T(8,128)S(1)} %reshape.31), channel_id=1, source_target_pairs={{0,16},{16,32},{32,48},{48,64},{64,80},{80,96},{96,112},{112,128},... | collective-permute-start | bytes 98312 | tf_op jit(solution)/shard_map/ppermute | solution.py:452
  15.3 6.6 %collective-permute-start.1 = (f32[8,1024]{1,0:T(8,128)S(1)}, f32[8,1024]{1,0:T(8,128)S(1)}, u32[]{:S(2)}, u32[]{:S(2)}) collective-permute-start(f32[8,1024]{1,0:T(8,128)S(1)} %reshape.32), channel_id=1, source_target_pairs={{16,0},{32,16},{48,32},{64,48},{80,64},{96,80},{112,96},{128,112},... | collective-permute-start | bytes 98312 | tf_op jit(solution)/shard_map/ppermute | solution.py:453
  24.4 0.9 %copy-start.2 = (f32[208,128]{1,0:T(8,128)S(1)}, f32[208,128]{1,0:T(8,128)}, u32[]{:S(2)}) copy-start(f32[208,128]{1,0:T(8,128)} %constant.5.clone.seed_ref) | copy-start | bytes 319492
  27.4 23.9 %all-to-all-start.1 = ((f32[32,16,128]{2,1,0:T(8,128)}), f32[32,16,128]{2,1,0:T(8,128)S(1)}, u32[]{:S(2)}, u32[]{:S(2)}) async-start(f32[32,16,128]{2,1,0:T(8,128)} %bitcast.3), calls=%async_computation.1 | async-start | bytes 524288 | tf_op jit(solution)/shard_map/all_to_all | solution.py:431
  37.1 25.3 %collective-permute-start.2 = (f32[1160,128]{1,0:T(8,128)S(1)}, f32[1160,128]{1,0:T(8,128)S(1)}, u32[]{:S(2)}, u32[]{:S(2)}) collective-permute-start(f32[1160,128]{1,0:T(8,128)S(1)} %get-tuple-element.4.r_ref.up_ref), channel_id=1, source_target_pairs={{0,1},{1,2},{2,3},{3,4},{4,5},{5,6},{6,7},{7,8},{8,9},{9,10},{10,1... | collective-permute-start | bytes 1781768 | tf_op jit(solution)/shard_map/ppermute | solution.py:460
  41.4 22.5 %collective-permute-start.3 = (f32[1160,128]{1,0:T(8,128)S(1)}, f32[1160,128]{1,0:T(8,128)S(1)}, u32[]{:S(2)}, u32[]{:S(2)}) collective-permute-start(f32[1160,128]{1,0:T(8,128)S(1)} %get-tuple-element.5.down_ref), channel_id=1, source_target_pairs={{1,0},{2,1},{3,2},{4,3},{5,4},{6,5},{7,6},{8,7},{9,8},{10,9},{11,1... | collective-permute-start | bytes 1781768 | tf_op jit(solution)/shard_map/ppermute | solution.py:461
  51.3 12.7 %copy-start.1 = (bf16[2,480,256]{2,1,0:T(8,128)(2,1)S(1)}, bf16[2,480,256]{2,1,0:T(8,128)(2,1)}, u32[]{:S(2)}) copy-start(bf16[2,480,256]{2,1,0:T(8,128)(2,1)} %constant.4.clone.b_ref) | copy-start | bytes 1474564

commit v3 on v2

--- a/solution.py
+++ b/solution.py
@@ -213,8 +213,7 @@
             ref[row + 36 : row + 40, :] = jnp.zeros((4, 128), F32)
 
 
-def spectral_kernel(r_ref, seed_ref, out_ref, fh_ref, fl_ref):
-    make_table(seed_ref, fh_ref, fl_ref)
+def spectral_kernel(r_ref, fh_ref, fl_ref, out_ref):
     spaced = synth_x(fh_ref, fl_ref, r_ref[0:BASE, :])
     halves = []
     for half in (spaced[:, :128], spaced[:, 128:]):
@@ -234,8 +233,7 @@
         out_ref[row : row + HALF, :] = o[:, :128] + sign_of((HALF, 128), 0) * o[:, 128:]
 
 
-def analysis_y_kernel(r_ref, seed_ref, out_ref, fh_ref, fl_ref):
-    make_table(seed_ref, fh_ref, fl_ref)
+def analysis_y_kernel(r_ref, fh_ref, fl_ref, out_ref):
     lane = lanes_of((16, 128))
     columns = []
     for t in range(6):
@@ -277,16 +275,14 @@
     down_ref,
     low_ref,
     high_ref,
-    seed_ref,
+    fh_ref,
+    fl_ref,
     b_ref,
     out_ref,
-    fh_ref,
-    fl_ref,
     x_ref,
     u_ref,
     s_ref,
 ):
-    make_table(seed_ref, fh_ref, fl_ref)
     below = low_ref[0:BASE, :]
     above = high_ref[0:BASE, :]
     left = lanes_of((BASE, 128)) < 64
@@ -452,6 +448,9 @@
     before = lax.ppermute(scalar[:, 30:32, :].reshape(8, 1024), "wa", up)
     after = lax.ppermute(scalar[:, 0:2, :].reshape(8, 1024), "wa", down)
 
+    quarter = of((N // 2, N // 2), BF16)
+    fh, fl = call(make_table, (quarter, quarter), 10**7, 8)(seeds)
+
     payload = of((PAYLOAD, 128), F32)
     to_up, to_down = call(pack_kernel, (payload, payload), 10**6, 8)(
         received, scalar, before, after
@@ -460,7 +459,9 @@
     from_low = lax.ppermute(to_up, "gz", up)
     from_high = lax.ppermute(to_down, "gz", down)
 
-    half = call(spectral_kernel, of((512, 128), F32), 10**9, 12, scratch=table)(to_up, seeds)
+    half = call(spectral_kernel, of((512, 128), F32), 10**9, 12)(
+        to_up, fh, fl
+    )
     returned = exchange(half)
 
     scalar_next = call(
@@ -468,16 +469,15 @@
         of((4, 32, 1024), F32),
         2 * 10**9,
         24,
-        scratch=table
-        + (
+        scratch=(
             pltpu.VMEM((3, N + 128, 128), F32),
             pltpu.VMEM((2, 8, 6 * EXT, 128), F32),
             pltpu.VMEM((6 * 8 * EXT + 8, 128), F32),
         ),
         smem=1,
-    )(nest_shift, to_up, to_down, from_low, from_high, seeds, stencil)
-
-    stress = call(analysis_y_kernel, of((64, 512), BF16), 10**9, 8, scratch=table)(returned, seeds)
+    )(nest_shift, to_up, to_down, from_low, from_high, fh, fl, stencil)
+
+    stress = call(analysis_y_kernel, of((64, 512), BF16), 10**9, 8)(returned, fh, fl)
     return (stress.reshape(2, 2, 16, 512), scalar_next)
 
 

time: 71.1 us -> 69.9 us (0.983)
  local copies, waits for them, and re-layouts: 0.89 us -> 0.1 us
    unnamed x6, local copies, waits for them, and re-layouts: 0.81 us -> 0.02 us
    pallas_call x5 -> x6, Pallas kernels: 12.6 us -> 12.2 us  [run(): pl.pallas_call(kernel, out_shape=outs, in_specs=specs, out_specs=jax.tree...]
  transfers between devices with their start and end apart: 6 -> 6, of which waited for: 5 -> 4; matrix products, arithmetic and copies ran while one was open for 0% -> 0% of each run, Pallas kernels for 2% -> 2%
where the time goes in v3:
time: 69.9 us; the launch traced here: 69.5 us
  starting transfers between devices  40.6 us (58%)
  waiting for transfers between devices  15.2 us (22%)
  Pallas kernels  12.2 us (17%)
  between operations  1.43 us (2%)
    all_to_all x2, starting transfers between devices, exchange(): lax.all_to_all(block, 'wa', split_axis=0, concat_axis=0, tiled=True)  20 us
    pallas_call x6, Pallas kernels, run(): pl.pallas_call(kernel, out_shape=outs, in_specs=specs, out_specs=jax.tree...  12.2 us
    ppermute x1, waiting for transfers between devices, shards(): from_low = lax.ppermute(to_up, 'gz', up)  9.87 us
    ppermute x1, starting transfers between devices, shards(): from_high = lax.ppermute(to_down, 'gz', down)  9.22 us
    ppermute x1, starting transfers between devices, shards(): after = lax.ppermute(scalar[:, 0:2, :].reshape(8, 1024), 'wa', down)  5.04 us
    ppermute x1, starting transfers between devices, shards(): from_low = lax.ppermute(to_up, 'gz', up)  4.28 us
    all_to_all x2, waiting for transfers between devices, exchange(): lax.all_to_all(block, 'wa', split_axis=0, concat_axis=0, tiled=True)  2.41 us
    ppermute x1, starting transfers between devices, shards(): before = lax.ppermute(scalar[:, 30:32, :].reshape(8, 1024), 'wa', up)  2.02 us
  transfers between devices with their start and end apart: 6, of which 4 were waited for; matrix products, arithmetic and copies ran while one was open for 0% of the time, Pallas kernels for 2%

profile of v3, /device:TPU:12, one launch (start us, length us, event | category | flops | bytes accessed | tf_op | source)
XLA Modules:
  0.0 69.5 jit_solution(9626812360620241013)
XLA Ops:
  0.6 2.3 %shard_map.68 = f32[512,128]{1,0:T(8,128)} custom-call(f32[64,512]{1,0:T(8,128)} %bitcast.9), custom_call_target="tpu_custom_call" | custom-call | flops 1000000000 | bytes 131072 | tf_op jit(solution)/shard_map/pallas_call | solution.py:403
  2.9 0.0 copy-start
  2.9 10.3 %all-to-all-start = ((f32[32,16,128]{2,1,0:T(8,128)}), f32[32,16,128]{2,1,0:T(8,128)S(1)}, u32[]{:S(2)}, u32[]{:S(2)}) async-start(f32[32,16,128]{2,1,0:T(8,128)} %bitcast.8), calls=%async_computation | async-start | bytes 524288 | tf_op jit(solution)/shard_map/all_to_all | solution.py:427
  13.2 0.0 copy-done
  13.2 0.0 copy-start.1
  13.3 2.0 %collective-permute-start = (f32[8,1024]{1,0:T(8,128)S(1)}, f32[8,1024]{1,0:T(8,128)S(1)}, u32[]{:S(2)}, u32[]{:S(2)}) collective-permute-start(f32[8,1024]{1,0:T(8,128)S(1)} %reshape.31), channel_id=1, source_target_pairs={{0,16},{16,32},{32,48},{48,64},{64,80},{80,96},{96,112},{112,128},... | collective-permute-start | bytes 98312 | tf_op jit(solution)/shard_map/ppermute | solution.py:448
  15.3 5.0 %collective-permute-start.1 = (f32[8,1024]{1,0:T(8,128)S(1)}, f32[8,1024]{1,0:T(8,128)S(1)}, u32[]{:S(2)}, u32[]{:S(2)}) collective-permute-start(f32[8,1024]{1,0:T(8,128)S(1)} %reshape.32), channel_id=1, source_target_pairs={{16,0},{32,16},{48,32},{64,48},{80,64},{96,80},{112,96},{128,112},... | collective-permute-start | bytes 98312 | tf_op jit(solution)/shard_map/ppermute | solution.py:449
  20.4 0.0 copy-done.1
  20.4 0.2 shard_map.70
  20.6 0.0 collective-permute-done.before_ref
  20.6 1.3 %collective-permute-done.1.after_ref = f32[8,1024]{1,0:T(8,128)S(1)} collective-permute-done((f32[8,1024]{1,0:T(8,128)S(1)}, f32[8,1024]{1,0:T(8,128)S(1)}, u32[]{:S(2)}, u32[]{:S(2)}) %collective-permute-start.1) | collective-permute-done | bytes 32800 | tf_op jit(solution)/shard_map/ppermute | solution.py:449
  22.0 2.4 %all-to-all-done = f32[32,16,128]{2,1,0:T(8,128)S(1)} async-done(((f32[32,16,128]{2,1,0:T(8,128)}), f32[32,16,128]{2,1,0:T(8,128)S(1)}, u32[]{:S(2)}, u32[]{:S(2)}) %all-to-all-start) | async-done | bytes 262176 | tf_op jit(solution)/shard_map/all_to_all | solution.py:427
  24.4 0.1 shard_map.69
  24.5 1.9 %shard_map.71 = f32[512,128]{1,0:T(8,128)} custom-call(f32[1160,128]{1,0:T(8,128)S(1)} %get-tuple-element.6.r_ref.up_ref, bf16[384,384]{1,0:T(8,128)(2,1)S(1)} %get-tuple-element.7.fh_ref, bf16[384,384]{1,0:T(8,128)(2,1)S(1)} %get-tuple-element.8.fl_ref), custom_call_target="tpu_custom_call" | custom-call | flops 1000000000 | bytes 1183744 | tf_op jit(solution)/shard_map/pallas_call | solution.py:403
  26.3 9.8 %all-to-all-start.1 = ((f32[32,16,128]{2,1,0:T(8,128)}), f32[32,16,128]{2,1,0:T(8,128)S(1)}, u32[]{:S(2)}, u32[]{:S(2)}) async-start(f32[32,16,128]{2,1,0:T(8,128)} %bitcast.3), calls=%async_computation.1 | async-start | bytes 524288 | tf_op jit(solution)/shard_map/all_to_all | solution.py:427
  36.1 4.3 %collective-permute-start.2 = (f32[1160,128]{1,0:T(8,128)S(1)}, f32[1160,128]{1,0:T(8,128)S(1)}, u32[]{:S(2)}, u32[]{:S(2)}) collective-permute-start(f32[1160,128]{1,0:T(8,128)S(1)} %get-tuple-element.6.r_ref.up_ref), channel_id=1, source_target_pairs={{0,1},{1,2},{2,3},{3,4},{4,5},{5,6},{6,7},{7,8},{8,9},{9,10},{10,1... | collective-permute-start | bytes 1781768 | tf_op jit(solution)/shard_map/ppermute | solution.py:459
  40.4 9.2 %collective-permute-start.3 = (f32[1160,128]{1,0:T(8,128)S(1)}, f32[1160,128]{1,0:T(8,128)S(1)}, u32[]{:S(2)}, u32[]{:S(2)}) collective-permute-start(f32[1160,128]{1,0:T(8,128)S(1)} %get-tuple-element.9.down_ref), channel_id=1, source_target_pairs={{1,0},{2,1},{3,2},{4,3},{5,4},{6,5},{7,6},{8,7},{9,8},{10,9},{11,1... | collective-permute-start | bytes 1781768 | tf_op jit(solution)/shard_map/ppermute | solution.py:460
  50.3 0.0 all-to-all-done.1
  50.3 0.0 copy-start.2
  50.3 1.2 %shard_map.72 = bf16[64,512]{1,0:T(8,128)(2,1)} custom-call(f32[512,128]{1,0:T(8,128)S(1)} %bitcast.7, bf16[384,384]{1,0:T(8,128)(2,1)S(1)} %get-tuple-element.7.fh_ref, bf16[384,384]{1,0:T(8,128)(2,1)S(1)} %get-tuple-element.8.fl_ref), custom_call_target="tpu_custom_call" | custom-call | flops 1000000000 | bytes 851968 | tf_op jit(solution)/shard_map/pallas_call | solution.py:403
  51.5 9.9 %collective-permute-done.2.low_ref = f32[1160,128]{1,0:T(8,128)S(1)} collective-permute-done((f32[1160,128]{1,0:T(8,128)S(1)}, f32[1160,128]{1,0:T(8,128)S(1)}, u32[]{:S(2)}, u32[]{:S(2)}) %collective-permute-start.2) | collective-permute-done | bytes 593952 | tf_op jit(solution)/shard_map/ppermute | solution.py:459
  61.4 1.6 %collective-permute-done.3.high_ref = f32[1160,128]{1,0:T(8,128)S(1)} collective-permute-done((f32[1160,128]{1,0:T(8,128)S(1)}, f32[1160,128]{1,0:T(8,128)S(1)}, u32[]{:S(2)}, u32[]{:S(2)}) %collective-permute-start.3) | collective-permute-done | bytes 593952 | tf_op jit(solution)/shard_map/ppermute | solution.py:460
  62.9 0.0 copy-done.2
  62.9 6.5 %shard_map.73 = f32[4,32,1024]{2,1,0:T(8,128)} custom-call(s32[1]{0:T(128)S(6)} %copy.7.shift_ref, f32[1160,128]{1,0:T(8,128)S(1)} %get-tuple-element.6.r_ref.up_ref, f32[1160,128]{1,0:T(8,128)S(1)} %get-tuple-element.9.down_ref, f32[1160,128]{1,0:T(8,128)S(1)} %collective-permute-done.2.low_ref, f32[1160,128]{1,0:T(8,128)S(1)} %collective-permute-done.3.high_ref, ...), custom_call_target="tpu_custom_call" | custom-call | flops 2000000000 | bytes 3457028 | tf_op jit(solution)/shard_map/pallas_call | solution.py:403
  (3 shorter events, 0.1 us)
Async XLA Ops:
  2.9 10.3 %copy-start = (f32[4,32,1024]{2,1,0:T(8,128)S(1)}, f32[4,32,1024]{2,1,0:T(8,128)}, u32[]{:S(2)}) copy-start(f32[4,32,1024]{2,1,0:T(8,128)} %g_ref.1) | copy-start | bytes 1572868
  2.9 21.4 %all-to-all-start = ((f32[32,16,128]{2,1,0:T(8,128)}), f32[32,16,128]{2,1,0:T(8,128)S(1)}, u32[]{:S(2)}, u32[]{:S(2)}) async-start(f32[32,16,128]{2,1,0:T(8,128)} %bitcast.8), calls=%async_computation | async-start | bytes 524288 | tf_op jit(solution)/shard_map/all_to_all | solution.py:427
  13.2 7.2 %copy-start.1 = (f32[208,128]{1,0:T(8,128)S(1)}, f32[208,128]{1,0:T(8,128)}, u32[]{:S(2)}) copy-start(f32[208,128]{1,0:T(8,128)} %constant.5.clone.seed_ref) | copy-start | bytes 319492
  13.3 7.4 %collective-permute-start = (f32[8,1024]{1,0:T(8,128)S(1)}, f32[8,1024]{1,0:T(8,128)S(1)}, u32[]{:S(2)}, u32[]{:S(2)}) collective-permute-start(f32[8,1024]{1,0:T(8,128)S(1)} %reshape.31), channel_id=1, source_target_pairs={{0,16},{16,32},{32,48},{48,64},{64,80},{80,96},{96,112},{112,128},... | collective-permute-start | bytes 98312 | tf_op jit(solution)/shard_map/ppermute | solution.py:448
  15.3 6.6 %collective-permute-start.1 = (f32[8,1024]{1,0:T(8,128)S(1)}, f32[8,1024]{1,0:T(8,128)S(1)}, u32[]{:S(2)}, u32[]{:S(2)}) collective-permute-start(f32[8,1024]{1,0:T(8,128)S(1)} %reshape.32), channel_id=1, source_target_pairs={{16,0},{32,16},{48,32},{64,48},{80,64},{96,80},{112,96},{128,112},... | collective-permute-start | bytes 98312 | tf_op jit(solution)/shard_map/ppermute | solution.py:449
  26.3 23.9 %all-to-all-start.1 = ((f32[32,16,128]{2,1,0:T(8,128)}), f32[32,16,128]{2,1,0:T(8,128)S(1)}, u32[]{:S(2)}, u32[]{:S(2)}) async-start(f32[32,16,128]{2,1,0:T(8,128)} %bitcast.3), calls=%async_computation.1 | async-start | bytes 524288 | tf_op jit(solution)/shard_map/all_to_all | solution.py:427
  36.1 25.3 %collective-permute-start.2 = (f32[1160,128]{1,0:T(8,128)S(1)}, f32[1160,128]{1,0:T(8,128)S(1)}, u32[]{:S(2)}, u32[]{:S(2)}) collective-permute-start(f32[1160,128]{1,0:T(8,128)S(1)} %get-tuple-element.6.r_ref.up_ref), channel_id=1, source_target_pairs={{0,1},{1,2},{2,3},{3,4},{4,5},{5,6},{6,7},{7,8},{8,9},{9,10},{10,1... | collective-permute-start | bytes 1781768 | tf_op jit(solution)/shard_map/ppermute | solution.py:459
  40.4 22.5 %collective-permute-start.3 = (f32[1160,128]{1,0:T(8,128)S(1)}, f32[1160,128]{1,0:T(8,128)S(1)}, u32[]{:S(2)}, u32[]{:S(2)}) collective-permute-start(f32[1160,128]{1,0:T(8,128)S(1)} %get-tuple-element.9.down_ref), channel_id=1, source_target_pairs={{1,0},{2,1},{3,2},{4,3},{5,4},{6,5},{7,6},{8,7},{9,8},{10,9},{11,1... | collective-permute-start | bytes 1781768 | tf_op jit(solution)/shard_map/ppermute | solution.py:460
  50.3 12.7 %copy-start.2 = (bf16[2,480,256]{2,1,0:T(8,128)(2,1)S(1)}, bf16[2,480,256]{2,1,0:T(8,128)(2,1)}, u32[]{:S(2)}) copy-start(bf16[2,480,256]{2,1,0:T(8,128)(2,1)} %constant.4.clone.b_ref) | copy-start | bytes 1474564
